TPU v7x, 256 devices: a whole 4x4x8 slice. The times are simulated.
256 devices in a mesh: req: 32 (over z, x), mlp: 8 (over y, core).
Axes of the slice: x: 4, y: 4, z: 8, core: 2. Of those that a mesh axis runs over, the one named last changes fastest.
Arguments:
- tokens: bfloat16 [8192, 2048], P('req', 'mlp'), may hold values from -12 to 12
- segment_ids: int32 [8192], P('req'), may hold values from 0 to 16, never falling along the last dimension, each value on 1 to 4096 neighbouring positions
- page_source: int32 [512], P('req'), may hold values from 0 to 511, each once
- query_weight: bfloat16 [2048, 2048], P(None, 'mlp')
- key_weight: bfloat16 [2048, 2048], P(None, 'mlp')
- value_weight: bfloat16 [2048, 2048], P(None, 'mlp'), may hold values from -0.125 to 0.125
- out_weight: bfloat16 [2048, 2048], P('mlp')
- query_gain: float32 [2048], P('mlp'), may hold values from 0.5 to 9
- key_gain: float32 [2048], P('mlp'), may hold values from 0.5 to 9
- attention_gain: float32 [2048], P('mlp'), may hold values from 0.25 to 1.75
- gate_weight: bfloat16 [2048, 8192], P('req', 'mlp'), may hold values from -0.125 to 0.125
- up_weight: bfloat16 [2048, 8192], P('req', 'mlp'), may hold values from -0.125 to 0.125
- down_weight: bfloat16 [2048, 8192], P('req', 'mlp')
- feedforward_gain: float32 [2048], P('mlp'), may hold values from 0.25 to 1.75
Outputs:
- layer_out: bfloat16 [8192, 2048], P('req', 'mlp')
- page_cache: bfloat16 [512, 2, 16, 2048], P('req', None, None, 'mlp')
Inputs may be any that keep to these rules, and one draw needn't show every extreme that they name: `segment_ids`: segment ids never fall along the stream; each prompt has 1 to 4096 tokens and one has exactly 4096. `page_source`: each stream page appears once.
All inputs are finite; a program needn't handle non-finite values.
Results may differ from a plain program's by a relative error of at most 0.019.
The roundings to bfloat16 on the way count: a program that leaves them out, or rounds other values in their place, can miss the bound.
Values may be sent and summed in bfloat16 or wider, within the bound.
No kernel may reach another device: no remote copies, remote signals or barrier semaphores. Data moves between devices by JAX's collectives and lax.ppermute only.
A program may use at most 128 MiB of HBM per device.

v0:
```python
import jax
import jax.numpy as jnp
from jax import lax
from jax.sharding import PartitionSpec as P

HD = 128
PAGE = 16


rope_base = 500000.0
norm_eps = 1e-06


def rope_tables(positions, head_dim):
    half_dim = head_dim // 2
    inv_freq = rope_base ** (-(jnp.arange(half_dim, dtype=jnp.float32) * 2.0) / head_dim)
    angles = positions.astype(jnp.float32)[:, None] * inv_freq[None, :]
    return (jnp.cos(angles), jnp.sin(angles))


def rotate(values, cosine_table, sine_table, head_dim):
    tok_rows = values.shape[0]
    head_count = values.shape[1] // head_dim
    shaped = values.reshape(tok_rows, head_count, head_dim)
    half_dim = head_dim // 2
    first_half = shaped[..., :half_dim]
    second = shaped[..., half_dim:]
    cos_b = cosine_table[:, None, :]
    sin_b = sine_table[:, None, :]
    turned = jnp.concatenate(
        [first_half * cos_b - second * sin_b, second * cos_b + first_half * sin_b], axis=-1
    )
    return turned.reshape(tok_rows, head_count * head_dim)


def post_norm(branch_term, gain_vec, model_width):
    own_part = lax.psum_scatter(
        branch_term.astype(jnp.bfloat16), "mlp", scatter_dimension=1, tiled=True
    ).astype(jnp.float32)
    mean_square = lax.psum(jnp.sum(own_part * own_part, axis=1), "mlp") / model_width
    return own_part * lax.rsqrt(mean_square + norm_eps)[:, None] * gain_vec[None, :]


def per_device(
    tokens,
    segment_ids,
    page_source,
    query_weight,
    key_weight,
    value_weight,
    out_weight,
    query_gain,
    key_gain,
    attention_gain,
    gate_weight,
    up_weight,
    down_weight,
    feedforward_gain,
):
    tok_rows = tokens.shape[0]
    local_width = tokens.shape[1]
    model_width = query_weight.shape[0]
    head_dim = HD
    head_count = local_width // head_dim
    full_rows = lax.all_gather(tokens, "mlp", axis=1, tiled=True)
    query_proj = jnp.dot(full_rows, query_weight, preferred_element_type=jnp.float32)
    key_proj = jnp.dot(full_rows, key_weight, preferred_element_type=jnp.float32)
    value_proj = jnp.dot(full_rows, value_weight, preferred_element_type=jnp.float32)
    query_total, key_total = lax.psum(
        (jnp.sum(query_proj * query_proj, axis=1), jnp.sum(key_proj * key_proj, axis=1)), "mlp"
    )
    query_n = (
        query_proj * lax.rsqrt(query_total / model_width + norm_eps)[:, None] * query_gain[None, :]
    )
    key_n = key_proj * lax.rsqrt(key_total / model_width + norm_eps)[:, None] * key_gain[None, :]
    seg_total = lax.axis_size("req") // 2 + 1
    seg_range = jnp.arange(seg_total, dtype=jnp.int32)
    matches = segment_ids[:, None] == seg_range[None, :]
    counts = jnp.sum(matches.astype(jnp.int32), axis=0)
    totals = lax.psum(counts, "req")
    seg_starts = jnp.cumsum(totals) - totals
    row_base = lax.axis_index("req") * tok_rows
    global_index = row_base + jnp.arange(tok_rows, dtype=jnp.int32)
    own_start = jnp.sum(jnp.where(matches, seg_starts[None, :], 0), axis=1)
    positions = global_index - own_start
    cosine_table, sine_table = rope_tables(positions, head_dim)
    query_r = rotate(query_n, cosine_table, sine_table, head_dim).astype(jnp.bfloat16)
    key_r = rotate(key_n, cosine_table, sine_table, head_dim).astype(jnp.bfloat16)
    value_b = value_proj.astype(jnp.bfloat16)
    query_heads = query_r.reshape(tok_rows, head_count, head_dim)
    score_scale = head_dim ** (-0.5)
    pages_here = page_source.shape[0]
    page_offsets = jnp.arange(PAGE, dtype=jnp.int32)
    attn_init = (
        jnp.full((head_count, tok_rows), -1e30, jnp.float32),
        jnp.zeros((head_count, tok_rows), jnp.float32),
        jnp.zeros((tok_rows, head_count, head_dim), jnp.float32),
    )
    cache_init = jnp.zeros((pages_here, 2, PAGE, local_width), jnp.bfloat16)
    fold_state = attn_init + (cache_init,)
    fetched = (
        lax.all_gather(key_r, "req", axis=0, tiled=True),
        lax.all_gather(value_b, "req", axis=0, tiled=True),
        lax.all_gather(segment_ids, "req", axis=0, tiled=True),
    )
    key_part, value_part, seg_part = fetched
    row_count = key_part.shape[0]
    block_rows = 512

    def one_block(block_index, state):
        run_max, run_sum, run_out = state
        offset = block_index * block_rows
        key_block = lax.dynamic_slice_in_dim(key_part, offset, block_rows, 0).reshape(
            block_rows, head_count, head_dim
        )
        value_block = lax.dynamic_slice_in_dim(value_part, offset, block_rows, 0).reshape(
            block_rows, head_count, head_dim
        )
        seg_block = lax.dynamic_slice_in_dim(seg_part, offset, block_rows, 0)
        key_index = offset + jnp.arange(block_rows, dtype=jnp.int32)
        visible = (
            (segment_ids[:, None] == seg_block[None, :])
            & (global_index[:, None] >= key_index[None, :])
            & (key_index[None, :] >= 0)
        )
        scores = (
            jnp.einsum("thd,rhd->htr", query_heads, key_block, preferred_element_type=jnp.float32)
            * score_scale
        )
        masked = jnp.where(visible[None], scores, -1e30)
        new_max = jnp.maximum(run_max, jnp.max(masked, axis=2))
        weights = jnp.where(visible[None], jnp.exp(scores - new_max[:, :, None]), 0.0)
        factor = jnp.exp(run_max - new_max)
        run_sum = run_sum * factor + jnp.sum(weights, axis=2)
        update = jnp.einsum(
            "htr,rhd->thd",
            weights.astype(jnp.bfloat16),
            value_block,
            preferred_element_type=jnp.float32,
        )
        run_out = run_out * factor.T[:, :, None] + update
        return (new_max, run_sum, run_out)

    attn_state = lax.fori_loop(0, row_count // block_rows, one_block, fold_state[:3])
    place_key_part = fetched[0]
    row_count = place_key_part.shape[0]
    page_rows = page_source[:, None] * PAGE + page_offsets[None, :]
    in_piece = (page_rows >= 0) & (page_rows < row_count)
    clipped = jnp.clip(page_rows, 0, row_count - 1)
    stacked = jnp.stack([place_key_part[clipped], fetched[1][clipped]], axis=1)
    page_cache = jnp.where(in_piece[:, None, :, None], stacked, fold_state[3])
    run_max, run_sum, run_out, page_cache = (
        attn_state[0],
        attn_state[1],
        attn_state[2],
        page_cache,
    )
    attended = (run_out / run_sum.T[:, :, None]).reshape(tok_rows, local_width).astype(jnp.bfloat16)
    projected = jnp.dot(attended, out_weight, preferred_element_type=jnp.float32)
    residual = (
        tokens.astype(jnp.float32) + post_norm(projected, attention_gain, model_width)
    ).astype(jnp.bfloat16)
    normed = lax.all_gather(residual, "mlp", axis=1, tiled=True)
    contract = (((1,), (1,)), ((), ()))
    fetched = (
        lax.all_gather(gate_weight, "req", axis=0, tiled=True),
        lax.all_gather(up_weight, "req", axis=0, tiled=True),
    )
    gate_act = jnp.dot(normed, fetched[0], preferred_element_type=jnp.float32)
    up_act = jnp.dot(normed, fetched[1], preferred_element_type=jnp.float32)
    hidden = (jax.nn.silu(gate_act) * up_act).astype(jnp.bfloat16)
    down_act = lax.dot_general(
        hidden,
        lax.all_gather(down_weight, "req", axis=0, tiled=True),
        contract,
        preferred_element_type=jnp.float32,
    )
    layer_out = (
        residual.astype(jnp.float32) + post_norm(down_act, feedforward_gain, model_width)
    ).astype(jnp.bfloat16)
    return (layer_out, page_cache)


def solution(mesh):
    in_specs = (
        P("req", "mlp"),
        P("req"),
        P("req"),
        P(None, "mlp"),
        P(None, "mlp"),
        P(None, "mlp"),
        P("mlp", None),
        P("mlp"),
        P("mlp"),
        P("mlp"),
        P("req", "mlp"),
        P("req", "mlp"),
        P("req", "mlp"),
        P("mlp"),
    )
    out_specs = (P("req", "mlp"), P("req", None, None, "mlp"))
    return jax.shard_map(
        per_device, mesh=mesh, in_specs=in_specs, out_specs=out_specs, check_vma=False
    )
```

profile of v0, /device:TPU:1, one launch (start us, length us, event | category | flops | bytes accessed | tf_op | source)
XLA Modules:
  0.0 639.1 jit_solution(3490800853905953545)
XLA Ops:
  8.8 19.9 %psum.36 = s32[17]{0:T(128)S(1)} all-reduce(s32[17]{0:T(128)S(1)} %convert_reduce_fusion), channel_id=1, replica_groups=mesh['req'=32,'mlp'=8] {'req'}, use_global_device_ids=true, to_apply=%region_3.0 | all-reduce | flops 17 | bytes 136 | tf_op jit(solution)/shard_map/psum | solution.py:80
  29.7 1.2 multiply_cosine_fusion
  30.9 9.1 %all-gather.9.cloned.1.call-done = bf16[256,2048]{1,0:T(8,128)(2,1)} async-done(((bf16[256,256]{1,0:T(8,128)(2,1)}), bf16[256,2048]{1,0:T(8,128)(2,1)}) %all-gather.9.cloned.1.call-update) | async-done | bytes 1048592 | tf_op jit(solution)/shard_map/all_gather | solution.py:65
  40.0 2.1 multiply_reduce_fusion.1
  42.1 2.2 multiply_reduce_fusion
  44.3 12.0 %all-reduce = (f32[256]{0:T(256)S(1)}, f32[256]{0:T(256)S(1)}) all-reduce(f32[256]{0:T(256)S(1)} %get-tuple-element.290, f32[256]{0:T(256)S(1)} %get-tuple-element.292), channel_id=1, replica_groups=mesh['req'=32,'mlp'=8] {'mlp'}, use_global_device_ids=true, to_apply=%region_1.0 | all-reduce | flops 512 | bytes 4096 | tf_op jit(solution)/shard_map/psum | solution.py:69
  59.1 2.3 convolution_convert_fusion.2
  61.5 35.7 %all-gather = s32[32,1,256]{2,1,0:T(1,128)S(1)} all-gather(s32[1,1,256]{2,1,0:T(1,128)S(1)} %bitcast.69), channel_id=1, replica_groups=mesh['req'=32,'mlp'=8] {'req'}, dimensions={0}, use_global_device_ids=true | all-gather | bytes 33792 | tf_op jit(solution)/shard_map/all_gather | solution.py:104
  97.3 41.7 %all-gather.11.cloned.1.call-done = bf16[8192,256]{1,0:T(8,128)(2,1)} async-done(((bf16[256,256]{1,0:T(8,128)(2,1)}), bf16[8192,256]{1,0:T(8,128)(2,1)}) %all-gather.11.cloned.1.call-update) | async-done | bytes 4194320 | tf_op jit(solution)/shard_map/all_gather | solution.py:102
  139.0 82.4 %all-gather.13.cloned.1.call-done = bf16[8192,256]{1,0:T(8,128)(2,1)} async-done(((bf16[256,256]{1,0:T(8,128)(2,1)}), bf16[8192,256]{1,0:T(8,128)(2,1)}) %all-gather.13.cloned.1.call-update) | async-done | bytes 4194320 | tf_op jit(solution)/shard_map/all_gather | solution.py:103
  221.4 44.8 %while.18 = (s32[]{:T(128)}, f32[2,256]{1,0:T(2,128)S(1)}, f32[2,256]{1,0:T(2,128)S(1)}, f32[256,2,128]{0,2,1:T(8,128)S(1)}, s32[256]{0:T(256)S(1)}, /*index=5*/...) while((s32[]{:T(128)}, f32[2,256]{1,0:T(2,128)S(1)}, ...), condition=%wide.region_11.12_spmd.clone, body=%wide.region_8.11_spmd.clone.sunk | while | flops 137302784 | bytes 6994131 | solution.py:144
  221.7 1.1 constant_dynamic-slice_fusion.3
  227.4 1.1 constant_dynamic-slice_fusion.3
  230.2 1.1 constant_dynamic-slice_fusion.3
  233.0 1.1 constant_dynamic-slice_fusion.3
  235.8 1.1 constant_dynamic-slice_fusion.3
  238.6 1.1 constant_dynamic-slice_fusion.3
  266.3 1.5 convolution_convert_fusion.1
  268.4 31.6 %reduce-scatter.3.cloned.1.call-done = bf16[256,256]{1,0:T(8,128)(2,1)} async-done(((bf16[256,2048]{1,0:T(8,128)(2,1)}), bf16[256,256]{1,0:T(8,128)(2,1)}) %reduce-scatter.3.cloned.1.call-update) | async-done | bytes 131088 | tf_op jit(solution)/shard_map/reduce_scatter | solution.py:37
  301.0 14.9 %psum.38 = f32[256]{0:T(256)S(1)} all-reduce(f32[256]{0:T(256)S(1)} %fusion.16), channel_id=1, replica_groups=mesh['req'=32,'mlp'=8] {'mlp'}, use_global_device_ids=true, to_apply=%region_14.15 | all-reduce | flops 256 | bytes 2048 | tf_op jit(solution)/shard_map/psum | solution.py:40
  315.9 1.7 fusion.19
  319.2 63.7 %all-gather.17.cloned.1.call-done = bf16[2048,1024]{1,0:T(8,128)(2,1)} async-done(((bf16[64,1024]{1,0:T(8,128)(2,1)}), bf16[2048,1024]{1,0:T(8,128)(2,1)}) %all-gather.17.cloned.1.call-update) | async-done | bytes 4194320 | tf_op jit(solution)/shard_map/all_gather | solution.py:166
  382.9 28.6 %all-gather.15.cloned.1.call-done = bf16[256,2048]{1,0:T(8,128)(2,1)} async-done(((bf16[256,256]{1,0:T(8,128)(2,1)}), bf16[256,2048]{1,0:T(8,128)(2,1)}) %all-gather.15.cloned.1.call-update) | async-done | bytes 1048592 | tf_op jit(solution)/shard_map/all_gather | solution.py:163
  411.5 3.8 fusion.31
  415.4 78.5 %all-gather.19.cloned.1.call-done = bf16[2048,1024]{1,0:T(8,128)(2,1)} async-done(((bf16[64,1024]{1,0:T(8,128)(2,1)}), bf16[2048,1024]{1,0:T(8,128)(2,1)}) %all-gather.19.cloned.1.call-update) | async-done | bytes 4194320 | tf_op jit(solution)/shard_map/all_gather | solution.py:167
  493.9 81.8 %all-gather.21.cloned.1.call-done = bf16[2048,1024]{1,0:T(8,128)(2,1)} async-done(((bf16[64,1024]{1,0:T(8,128)(2,1)}), bf16[2048,1024]{1,0:T(8,128)(2,1)}) %all-gather.21.cloned.1.call-update) | async-done | bytes 4194320 | tf_op jit(solution)/shard_map/all_gather | solution.py:174
  575.6 7.1 %convolution_convert_fusion = bf16[256,2048]{1,0:T(8,128)(2,1)} fusion(bf16[2048,1024]{1,0:T(8,128)(2,1)} %all-gather.21.cloned.1.call-done, bf16[256,2048]{1,0:T(8,128)(2,1)S(1)} %copy-done.9, bf16[2048,1024]{1,0:T(8,128)(2,1)} %all-gather.19.cloned.1.call-done, f32[256,1024]{1,0:T(8,128)S(1)} %fusion.31), kind=kOutput, calls=%fused_computation.28 | convolution fusion | flops 2149580800 | bytes 11534336 | tf_op jit(solution)/shard_map/dot_general | solution.py:172
  583.0 3.7 gather_fusion
  586.7 3.7 gather_fusion.1
  591.2 23.7 %reduce-scatter.5.cloned.1.call-done = bf16[256,256]{1,0:T(8,128)(2,1)} async-done(((bf16[256,2048]{1,0:T(8,128)(2,1)}), bf16[256,256]{1,0:T(8,128)(2,1)}) %reduce-scatter.5.cloned.1.call-update) | async-done | bytes 131088 | tf_op jit(solution)/shard_map/reduce_scatter | solution.py:37
  616.0 14.9 %psum.39 = f32[256]{0:T(256)S(1)} all-reduce(f32[256]{0:T(256)S(1)} %fusion.20), channel_id=1, replica_groups=mesh['req'=32,'mlp'=8] {'mlp'}, use_global_device_ids=true, to_apply=%region_17.18 | all-reduce | flops 256 | bytes 2048 | tf_op jit(solution)/shard_map/psum | solution.py:40
  630.9 1.7 fusion.23
  (292 shorter events, 47.8 us)
Async XLA Ops:
  7.2 259.1 %copy-start = (bf16[256,2048]{1,0:T(8,128)(2,1)S(1)}, bf16[256,2048]{1,0:T(8,128)(2,1)}, u32[]{:S(2)}) copy-start(bf16[256,2048]{1,0:T(8,128)(2,1)} %param.22) | copy-start | bytes 3145732
  7.2 49.2 %copy-start.5 = (f32[256]{0:T(256)S(1)}, f32[256]{0:T(256)}, u32[]{:S(2)}) copy-start(f32[256]{0:T(256)} %param.24) | copy-start | bytes 3076
  7.2 49.6 %copy-start.6 = (f32[256]{0:T(256)S(1)}, f32[256]{0:T(256)}, u32[]{:S(2)}) copy-start(f32[256]{0:T(256)} %param.23) | copy-start | bytes 3076
  7.2 32.8 %all-gather.9.cloned.1.call-start = ((), (), s32[]{:S(2)}) async-start(), calls=%async_computation.2 | async-start | bytes 1179648 | tf_op jit(solution)/shard_map/all_gather | solution.py:65
  7.9 131.1 %all-gather.11.cloned.1.call-start = ((), (), s32[]{:S(2)}) async-start(), calls=%async_computation.3 | async-start | bytes 4325376 | tf_op jit(solution)/shard_map/all_gather | solution.py:102
  42.1 16.9 %copy-start.1 = (bf16[256,2048]{1,0:T(8,128)(2,1)S(1)}, bf16[256,2048]{1,0:T(8,128)(2,1)}, u32[]{:S(2)}) copy-start(bf16[256,2048]{1,0:T(8,128)(2,1)} %all-gather.9.cloned.1.call-done) | copy-start | bytes 3145732
  56.4 5.1 copy-start.4
  59.0 162.4 %all-gather.13.cloned.1.call-start = ((), (), s32[]{:S(2)}) async-start(), calls=%async_computation.4 | async-start | bytes 4325376 | tf_op jit(solution)/shard_map/all_gather | solution.py:103
  61.4 238.6 %reduce-scatter.3.cloned.1.call-start = ((), (), s32[]{:S(2)}) async-start(), calls=%async_computation.5 | async-start | bytes 1179648 | tf_op jit(solution)/shard_map/reduce_scatter | solution.py:37
  221.4 94.6 %copy-start.3 = (bf16[256,256]{1,0:T(8,128)(2,1)S(1)}, bf16[256,256]{1,0:T(8,128)(2,1)}, u32[]{:S(2)}) copy-start(bf16[256,256]{1,0:T(8,128)(2,1)} %param.16) | copy-start | bytes 393220
  221.4 94.6 %copy-start.7 = (f32[256]{0:T(256)S(1)}, f32[256]{0:T(256)}, u32[]{:S(2)}) copy-start(f32[256]{0:T(256)} %param.25) | copy-start | bytes 3076
  267.8 115.1 %all-gather.17.cloned.1.call-start = ((), (), s32[]{:S(2)}) async-start(), calls=%async_computation.7 | async-start | bytes 4325376 | tf_op jit(solution)/shard_map/all_gather | solution.py:166
  268.4 143.1 %all-gather.15.cloned.1.call-start = ((), (), s32[]{:S(2)}) async-start(), calls=%async_computation.6 | async-start | bytes 1179648 | tf_op jit(solution)/shard_map/all_gather | solution.py:163
  317.6 176.2 %all-gather.19.cloned.1.call-start = ((), (), s32[]{:S(2)}) async-start(), calls=%async_computation.8 | async-start | bytes 4325376 | tf_op jit(solution)/shard_map/all_gather | solution.py:167
  318.4 257.2 %all-gather.21.cloned.1.call-start = ((), (), s32[]{:S(2)}) async-start(), calls=%async_computation.9 | async-start | bytes 4325376 | tf_op jit(solution)/shard_map/all_gather | solution.py:174
  319.1 295.8 %reduce-scatter.5.cloned.1.call-start = ((), (), s32[]{:S(2)}) async-start(), calls=%async_computation.10 | async-start | bytes 1179648 | tf_op jit(solution)/shard_map/reduce_scatter | solution.py:37
  411.5 164.1 %copy-start.9 = (bf16[256,2048]{1,0:T(8,128)(2,1)S(1)}, bf16[256,2048]{1,0:T(8,128)(2,1)}, u32[]{:S(2)}) copy-start(bf16[256,2048]{1,0:T(8,128)(2,1)} %all-gather.15.cloned.1.call-done) | copy-start | bytes 3145732
  415.4 167.4 %copy-start.10 = (s32[16]{0:T(128)S(1)}, s32[16]{0:T(128)}, u32[]{:S(2)}) copy-start(s32[16]{0:T(128)} %param.18) | copy-start | bytes 196
  415.4 215.5 %copy-start.8 = (f32[256]{0:T(256)S(1)}, f32[256]{0:T(256)}, u32[]{:S(2)}) copy-start(f32[256]{0:T(256)} %param.29) | copy-start | bytes 3076
  582.7 48.2 %copy-start.2 = (bf16[256,256]{1,0:T(8,128)(2,1)S(1)}, bf16[256,256]{1,0:T(8,128)(2,1)}, u32[]{:S(2)}) copy-start(bf16[256,256]{1,0:T(8,128)(2,1)} %fusion.19) | copy-start | bytes 393220
Sparse Core Ops, SparseCore 0:
  9.9 30.1 all-gather.8
  59.1 79.8 all-gather.10
  142.2 79.1 all-gather.12
  267.9 32.0 reduce-scatter.2
  302.4 80.4 all-gather.16
  385.1 26.3 all-gather.14
  414.1 79.7 all-gather.18
  496.4 79.1 all-gather.20
  582.9 32.0 reduce-scatter.4
where the time goes:
time: 640 us; the launch traced here: 639 us
  waiting for transfers between devices  444 us (69%)
  blocking collectives  97.4 us (15%)
  local copies, waits for them, and re-layouts  31.1 us (5%)
  matrix products  31 us (5%)
  other arithmetic  20.1 us (3%)
  between operations  14.1 us (2%)
    all_gather x1, waiting for transfers between devices, per_device(): lax.all_gather(value_b, 'req', axis=0, tiled=True)  82.4 us
    all_gather x1, waiting for transfers between devices, per_device(): lax.all_gather(down_weight, 'req', axis=0, tiled=True)  81.8 us
    all_gather x1, waiting for transfers between devices, per_device(): lax.all_gather(up_weight, 'req', axis=0, tiled=True)  78.5 us
    all_gather x1, waiting for transfers between devices, per_device(): lax.all_gather(gate_weight, 'req', axis=0, tiled=True)  63.7 us
    reduce_scatter x2, waiting for transfers between devices, post_norm(): lax.psum_scatter(branch_term.astype(jnp.bfloat16), 'mlp', scatter_dimensi...  55.3 us
    all_gather x1, waiting for transfers between devices, per_device(): lax.all_gather(key_r, 'req', axis=0, tiled=True)  41.7 us
    all_gather x1, blocking collectives, per_device(): lax.all_gather(segment_ids, 'req', axis=0, tiled=True)  35.7 us
    psum x2, blocking collectives, post_norm(): lax.psum(jnp.sum(own_part * own_part, axis=1), 'mlp') / model_width  29.8 us
  transfers between devices with their start and end apart: 9, of which 9 were waited for; matrix products, arithmetic and copies ran while one was open for 3% of the time, Pallas kernels for 0%

commit v1 on v0

--- a/solution.py
+++ b/solution.py
@@ -5,6 +5,10 @@
 
 HD = 128
 PAGE = 16
+ZS = 8
+XS = 4
+YS = 4
+RINGS = ZS * XS
 
 
 rope_base = 500000.0
@@ -33,11 +37,121 @@
     return turned.reshape(tok_rows, head_count * head_dim)
 
 
+def ring_shift(size, stride, step):
+    pairs = []
+    for src in range(RINGS):
+        place = (src // stride) % size
+        pairs.append((src, src + ((place + step) % size - place) * stride))
+    return pairs
+
+
+def ring_place(size, stride):
+    return (lax.axis_index("req") // stride) % size
+
+
+def ring_gather(piece, size, stride, put, state):
+    place = ring_place(size, stride)
+    state = put(state, piece, place, 0)
+    ahead = behind = piece
+    for step in range(1, size // 2):
+        ahead = lax.ppermute(ahead, "req", ring_shift(size, stride, 1))
+        behind = lax.ppermute(behind, "req", ring_shift(size, stride, -1))
+        state = put(state, ahead, (place - step) % size, 0)
+        state = put(state, behind, (place + step) % size, 0)
+    half = piece.shape[0] // 2
+    ahead = lax.ppermute(ahead[:half], "req", ring_shift(size, stride, 1))
+    behind = lax.ppermute(behind[half:], "req", ring_shift(size, stride, -1))
+    far = (place + size // 2) % size
+    state = put(state, ahead, far, 0)
+    return put(state, behind, far, half)
+
+
+def gather_req(piece, z_first):
+    rows, cols = piece.shape
+
+    def put_line(state, part, place, row):
+        return lax.dynamic_update_slice(state, part[None], (place, row, 0))
+
+    def put_z(state, part, place, row):
+        return lax.dynamic_update_slice(state, part[None], (place, row, 0, 0))
+
+    def put_x(state, part, place, row):
+        return lax.dynamic_update_slice(state, part[:, None], (row, place, 0, 0))
+
+    whole = jnp.zeros((ZS, XS, rows, cols), piece.dtype)
+    if z_first:
+        line = ring_gather(piece, ZS, XS, put_line, jnp.zeros((ZS, rows, cols), piece.dtype))
+        whole = ring_gather(line, XS, 1, put_x, whole)
+    else:
+        line = ring_gather(piece, XS, 1, put_line, jnp.zeros((XS, rows, cols), piece.dtype))
+        whole = ring_gather(line, ZS, XS, put_z, whole)
+    return whole.reshape(RINGS * rows, cols)
+
+
+def gather_ids(segment_ids):
+    rows = segment_ids.shape[0]
+    own_z = ring_place(ZS, XS)
+    own_x = ring_place(XS, 1)
+    line = jnp.zeros((ZS, rows), jnp.int32)
+    for step in range(ZS):
+        part = lax.ppermute(segment_ids, "req", ring_shift(ZS, XS, step)) if step else segment_ids
+        line = lax.dynamic_update_slice(line, part[None], ((own_z - step) % ZS, 0))
+    whole = jnp.zeros((ZS, XS, rows), jnp.int32)
+    for step in range(XS):
+        part = lax.ppermute(line, "req", ring_shift(XS, 1, step)) if step else line
+        whole = lax.dynamic_update_slice(whole, part[:, None], (0, (own_x - step) % XS, 0))
+    return whole.reshape(-1)
+
+
+def mlp_pairs(dy, dc):
+    return [(m, ((m // 2 + dy) % YS) * 2 + (m % 2 ^ dc)) for m in range(2 * YS)]
+
+
+def mlp_sum(values):
+    total = values
+    for dy in range(YS):
+        for dc in range(2):
+            if dy or dc:
+                total = total + lax.ppermute(values, "mlp", mlp_pairs(dy, dc))
+    return total
+
+
+def mlp_gather(piece):
+    rows, width = piece.shape
+    own = lax.axis_index("mlp")
+    own_y, own_c = own // 2, own % 2
+    whole = jnp.zeros((rows, width * 2 * YS), piece.dtype)
+    for dy in range(YS):
+        part = lax.ppermute(piece, "mlp", mlp_pairs(dy, 0)) if dy else piece
+        other = lax.ppermute(part, "mlp", mlp_pairs(0, 1))
+        src_y = (own_y - dy) % YS
+        whole = lax.dynamic_update_slice(whole, part, (0, (src_y * 2 + own_c) * width))
+        whole = lax.dynamic_update_slice(whole, other, (0, (src_y * 2 + 1 - own_c) * width))
+    return whole
+
+
+def mlp_scatter_sum(values):
+    rows = values.shape[0]
+    width = values.shape[1] // (2 * YS)
+    own = lax.axis_index("mlp")
+    own_y, own_c = own // 2, own % 2
+    total = None
+    for dy in (2, 1, 3, 0):
+        dst_y = (own_y + dy) % YS
+        theirs = lax.dynamic_slice(values, (0, (dst_y * 2 + 1 - own_c) * width), (rows, width))
+        mine = lax.dynamic_slice(values, (0, (dst_y * 2 + own_c) * width), (rows, width))
+        got = lax.ppermute(theirs.astype(jnp.bfloat16), "mlp", mlp_pairs(0, 1))
+        pair = mine + got.astype(jnp.float32)
+        if dy:
+            pair = lax.ppermute(pair.astype(jnp.bfloat16), "mlp", mlp_pairs(dy, 0))
+            pair = pair.astype(jnp.float32)
+        total = pair if total is None else total + pair
+    return total
+
+
 def post_norm(branch_term, gain_vec, model_width):
-    own_part = lax.psum_scatter(
-        branch_term.astype(jnp.bfloat16), "mlp", scatter_dimension=1, tiled=True
-    ).astype(jnp.float32)
-    mean_square = lax.psum(jnp.sum(own_part * own_part, axis=1), "mlp") / model_width
+    own_part = mlp_scatter_sum(branch_term)
+    mean_square = mlp_sum(jnp.sum(own_part * own_part, axis=1)) / model_width
     return own_part * lax.rsqrt(mean_square + norm_eps)[:, None] * gain_vec[None, :]
 
 
@@ -62,12 +176,22 @@
     model_width = query_weight.shape[0]
     head_dim = HD
     head_count = local_width // head_dim
-    full_rows = lax.all_gather(tokens, "mlp", axis=1, tiled=True)
+    half_units = gate_weight.shape[1] // 2
+    ffn_low = gather_req(
+        jnp.concatenate([w[:, :half_units] for w in (gate_weight, up_weight, down_weight)], axis=1),
+        True,
+    )
+    ffn_high = gather_req(
+        jnp.concatenate([w[:, half_units:] for w in (gate_weight, up_weight, down_weight)], axis=1),
+        False,
+    )
+    seg_part = gather_ids(segment_ids)
+    full_rows = mlp_gather(tokens)
     query_proj = jnp.dot(full_rows, query_weight, preferred_element_type=jnp.float32)
     key_proj = jnp.dot(full_rows, key_weight, preferred_element_type=jnp.float32)
     value_proj = jnp.dot(full_rows, value_weight, preferred_element_type=jnp.float32)
-    query_total, key_total = lax.psum(
-        (jnp.sum(query_proj * query_proj, axis=1), jnp.sum(key_proj * key_proj, axis=1)), "mlp"
+    query_total, key_total = mlp_sum(
+        jnp.stack([jnp.sum(query_proj * query_proj, axis=1), jnp.sum(key_proj * key_proj, axis=1)])
     )
     query_n = (
         query_proj * lax.rsqrt(query_total / model_width + norm_eps)[:, None] * query_gain[None, :]
@@ -76,9 +200,7 @@
     seg_total = lax.axis_size("req") // 2 + 1
     seg_range = jnp.arange(seg_total, dtype=jnp.int32)
     matches = segment_ids[:, None] == seg_range[None, :]
-    counts = jnp.sum(matches.astype(jnp.int32), axis=0)
-    totals = lax.psum(counts, "req")
-    seg_starts = jnp.cumsum(totals) - totals
+    seg_starts = jnp.sum((seg_part[:, None] < seg_range[None, :]).astype(jnp.int32), axis=0)
     row_base = lax.axis_index("req") * tok_rows
     global_index = row_base + jnp.arange(tok_rows, dtype=jnp.int32)
     own_start = jnp.sum(jnp.where(matches, seg_starts[None, :], 0), axis=1)
@@ -96,14 +218,8 @@
         jnp.zeros((head_count, tok_rows), jnp.float32),
         jnp.zeros((tok_rows, head_count, head_dim), jnp.float32),
     )
-    cache_init = jnp.zeros((pages_here, 2, PAGE, local_width), jnp.bfloat16)
-    fold_state = attn_init + (cache_init,)
-    fetched = (
-        lax.all_gather(key_r, "req", axis=0, tiled=True),
-        lax.all_gather(value_b, "req", axis=0, tiled=True),
-        lax.all_gather(segment_ids, "req", axis=0, tiled=True),
-    )
-    key_part, value_part, seg_part = fetched
+    fetched = (gather_req(key_r, True), gather_req(value_b, False))
+    key_part, value_part = fetched
     row_count = key_part.shape[0]
     block_rows = 512
 
@@ -141,40 +257,32 @@
         run_out = run_out * factor.T[:, :, None] + update
         return (new_max, run_sum, run_out)
 
-    attn_state = lax.fori_loop(0, row_count // block_rows, one_block, fold_state[:3])
-    place_key_part = fetched[0]
-    row_count = place_key_part.shape[0]
+    first_block = own_start[0] // block_rows
+    last_block = (row_base + tok_rows + block_rows - 1) // block_rows
+    attn_state = lax.fori_loop(first_block, last_block, one_block, attn_init)
     page_rows = page_source[:, None] * PAGE + page_offsets[None, :]
-    in_piece = (page_rows >= 0) & (page_rows < row_count)
-    clipped = jnp.clip(page_rows, 0, row_count - 1)
-    stacked = jnp.stack([place_key_part[clipped], fetched[1][clipped]], axis=1)
-    page_cache = jnp.where(in_piece[:, None, :, None], stacked, fold_state[3])
-    run_max, run_sum, run_out, page_cache = (
-        attn_state[0],
-        attn_state[1],
-        attn_state[2],
-        page_cache,
-    )
+    page_cache = jnp.stack([key_part[page_rows], value_part[page_rows]], axis=1)
+    run_max, run_sum, run_out = attn_state
     attended = (run_out / run_sum.T[:, :, None]).reshape(tok_rows, local_width).astype(jnp.bfloat16)
     projected = jnp.dot(attended, out_weight, preferred_element_type=jnp.float32)
     residual = (
         tokens.astype(jnp.float32) + post_norm(projected, attention_gain, model_width)
     ).astype(jnp.bfloat16)
-    normed = lax.all_gather(residual, "mlp", axis=1, tiled=True)
+    normed = mlp_gather(residual)
     contract = (((1,), (1,)), ((), ()))
-    fetched = (
-        lax.all_gather(gate_weight, "req", axis=0, tiled=True),
-        lax.all_gather(up_weight, "req", axis=0, tiled=True),
-    )
-    gate_act = jnp.dot(normed, fetched[0], preferred_element_type=jnp.float32)
-    up_act = jnp.dot(normed, fetched[1], preferred_element_type=jnp.float32)
-    hidden = (jax.nn.silu(gate_act) * up_act).astype(jnp.bfloat16)
-    down_act = lax.dot_general(
-        hidden,
-        lax.all_gather(down_weight, "req", axis=0, tiled=True),
-        contract,
-        preferred_element_type=jnp.float32,
-    )
+    down_act = None
+    for part in (ffn_low, ffn_high):
+        gate_act = jnp.dot(
+            normed, part[:, :half_units], preferred_element_type=jnp.float32
+        )
+        up_act = jnp.dot(
+            normed, part[:, half_units : 2 * half_units], preferred_element_type=jnp.float32
+        )
+        hidden = (jax.nn.silu(gate_act) * up_act).astype(jnp.bfloat16)
+        down = lax.dot_general(
+            hidden, part[:, 2 * half_units :], contract, preferred_element_type=jnp.float32
+        )
+        down_act = down if down_act is None else down_act + down
     layer_out = (
         residual.astype(jnp.float32) + post_norm(down_act, feedforward_gain, model_width)
     ).astype(jnp.bfloat16)

time: 640 us -> 391 us (0.61)
  waiting for transfers between devices: 444 us -> 83.1 us
  starting transfers between devices: 0.36 us -> 168 us
  blocking collectives: 97.4 us -> 0 us
  local copies, waits for them, and re-layouts: 31.1 us -> 100 us
  matrix products: 31 us -> 19.8 us
  other arithmetic: 20.1 us -> 8.92 us
  between operations: 14.1 us -> 4.65 us
    all_gather x7 -> x0, waiting for transfers between devices: 386 us -> none  [the longest x1 82.4 us: per_device(): lax.all_gather(value_b, 'req', axis=0, tiled=True)]
    ppermute x0 -> x107, starting transfers between devices: none -> 168 us  [the longest x8 44 us: ring_gather(): behind = lax.ppermute(behind[half:], 'req', ring_shift(size, stride, -1))]
    ppermute x0 -> x107, waiting for transfers between devices: none -> 83.1 us  [the longest x8 32.6 us: ring_gather(): ahead = lax.ppermute(ahead[:half], 'req', ring_shift(size, stride, 1))]
    psum x4 -> x0, blocking collectives: 61.7 us -> none  [the longest x2 29.8 us: post_norm(): lax.psum(jnp.sum(own_part * own_part, axis=1), 'mlp') / model_width]
    dynamic_update_slice x0 -> x80, local copies, waits for them, and re-layouts: none -> 56.1 us  [the longest x18 22.1 us: put_z(): return lax.dynamic_update_slice(state, part[None], (place, row, 0, 0))]
    reduce_scatter x2 -> x0, waiting for transfers between devices: 55.3 us -> none  [post_norm(): lax.psum_scatter(branch_term.astype(jnp.bfloat16), 'mlp', scatter_dimensi...]
    all_gather x1 -> x0, blocking collectives: 35.7 us -> none  [per_device(): lax.all_gather(segment_ids, 'req', axis=0, tiled=True)]
    dynamic_slice x32 -> x2, local copies, waits for them, and re-layouts: 19.4 us -> 1.21 us  [one_block(): lax.dynamic_slice_in_dim(value_part, offset, block_rows, 0)]
  transfers between devices with their start and end apart: 9 -> 107, of which waited for: 9 -> 20; matrix products, arithmetic and copies ran while one was open for 3% -> 29% of each run, Pallas kernels for 0% -> 0%
where the time goes in v1:
time: 391 us; the launch traced here: 385 us
  starting transfers between devices  168 us (43%)
  local copies, waits for them, and re-layouts  100 us (26%)
  waiting for transfers between devices  83.1 us (21%)
  matrix products  19.8 us (5%)
  other arithmetic  8.92 us (2%)
  between operations  4.65 us (1%)
    ppermute x8, starting transfers between devices, ring_gather(): behind = lax.ppermute(behind[half:], 'req', ring_shift(size, stride, -1))  44 us
    ppermute x8, waiting for transfers between devices, ring_gather(): ahead = lax.ppermute(ahead[:half], 'req', ring_shift(size, stride, 1))  32.6 us
    ppermute x21, starting transfers between devices, mlp_sum(): total = total + lax.ppermute(values, 'mlp', mlp_pairs(dy, dc))  27.9 us
    ppermute x16, starting transfers between devices, ring_gather(): behind = lax.ppermute(behind, 'req', ring_shift(size, stride, -1))  24.2 us
    ppermute x16, waiting for transfers between devices, ring_gather(): ahead = lax.ppermute(ahead, 'req', ring_shift(size, stride, 1))  22.6 us
    dynamic_update_slice x18, local copies, waits for them, and re-layouts, put_z(): return lax.dynamic_update_slice(state, part[None], (place, row, 0, 0))  22.1 us
    dynamic_update_slice x25, local copies, waits for them, and re-layouts, put_line(): return lax.dynamic_update_slice(state, part[None], (place, row, 0))  19.9 us
    ppermute x16, waiting for transfers between devices, ring_gather(): behind = lax.ppermute(behind, 'req', ring_shift(size, stride, -1))  17.6 us
  transfers between devices with their start and end apart: 107, of which 20 were waited for; matrix products, arithmetic and copies ran while one was open for 29% of the time, Pallas kernels for 0%

profile of v1, /device:TPU:1, one launch (start us, length us, event | category | flops | bytes accessed | tf_op | source)
XLA Modules:
  0.0 384.9 jit_solution(13519009662442395500)
XLA Ops:
  3.2 3.0 collective-permute-start.1
  6.2 3.8 collective-permute-start.2
  10.4 4.5 %collective-permute-start.4 = (s32[256]{0:T(256)}, s32[256]{0:T(256)S(1)}, u32[]{:S(2)}, u32[]{:S(2)}) collective-permute-start(s32[256]{0:T(256)} %param.17), channel_id=1, source_target_pairs={{0,160},{8,168},{16,176},{24,184},{32,192},{40,200},{48,208},{56,2... | collective-permute-start | bytes 3080 | tf_op jit(solution)/shard_map/ppermute | solution.py:97
  51.4 3.3 collective-permute-start.12
  65.8 2.8 collective-permute-start.20
  74.5 11.2 %collective-permute-start.84 = (bf16[32,1536]{1,0:T(8,128)(2,1)}, bf16[32,1536]{1,0:T(8,128)(2,1)}, u32[]{:S(2)}, u32[]{:S(2)}) collective-permute-start(bf16[32,1536]{1,0:T(8,128)(2,1)} %slice.156), channel_id=1, source_target_pairs={{0,24},{8,0},{16,8},{24,16},{32,56},{40,32},{48,40},{56,48},{64,88... | collective-permute-start | bytes 294920 | tf_op jit(solution)/shard_map/ppermute | solution.py:63
  89.1 2.8 collective-permute-start.37
  93.7 3.3 broadcast.262.clone
  124.3 4.0 %collective-permute-done.26 = bf16[256,256]{0,1:T(8,128)(2,1)S(1)} collective-permute-done((bf16[256,256]{0,1:T(8,128)(2,1)}, bf16[256,256]{0,1:T(8,128)(2,1)S(1)}, u32[]{:S(2)}, u32[]{:S(2)}) %collective-permute-start.26) | collective-permute-done | bytes 131104 | tf_op jit(solution)/shard_map/ppermute | solution.py:57
  138.0 5.7 %collective-permute-done.28 = bf16[256,256]{0,1:T(8,128)(2,1)S(1)} collective-permute-done((bf16[256,256]{0,1:T(8,128)(2,1)}, bf16[256,256]{0,1:T(8,128)(2,1)S(1)}, u32[]{:S(2)}, u32[]{:S(2)}) %collective-permute-start.28) | collective-permute-done | bytes 131104 | tf_op jit(solution)/shard_map/ppermute | solution.py:57
  154.9 3.4 broadcast.262.clone.1
  167.0 2.8 collective-permute-start.33
  177.3 4.2 %collective-permute-done.42 = bf16[4,256,256]{2,1,0:T(8,128)(2,1)S(1)} collective-permute-done((bf16[4,256,256]{2,1,0:T(8,128)(2,1)}, bf16[4,256,256]{2,1,0:T(8,128)(2,1)S(1)}, u32[]{:S(2)}, u32[]{:S(2)}) %collective-permute-start.42) | collective-permute-done | bytes 524320 | tf_op jit(solution)/shard_map/ppermute | solution.py:57
  183.5 3.9 %collective-permute-done.32 = bf16[8,256,256]{2,1,0:T(8,128)(2,1)S(1)} collective-permute-done((bf16[8,256,256]{2,1,0:T(8,128)(2,1)S(1)}, bf16[8,256,256]{2,1,0:T(8,128)(2,1)S(1)}, u32[]{:S(2)}, u32[]{:S(2)}) %collective-permute-start.32) | collective-permute-done | bytes 1048608 | tf_op jit(solution)/shard_map/ppermute | solution.py:57
  188.1 4.9 %collective-permute-done.44 = bf16[4,256,256]{2,1,0:T(8,128)(2,1)S(1)} collective-permute-done((bf16[4,256,256]{2,1,0:T(8,128)(2,1)S(1)}, bf16[4,256,256]{2,1,0:T(8,128)(2,1)S(1)}, u32[]{:S(2)}, u32[]{:S(2)}) %collective-permute-start.44) | collective-permute-done | bytes 524320 | tf_op jit(solution)/shard_map/ppermute | solution.py:57
  199.0 3.5 collective-permute-done.46
  205.8 26.6 %collective-permute-done.34 = bf16[4,256,256]{2,1,0:T(8,128)(2,1)S(1)} collective-permute-done((bf16[4,256,256]{2,1,0:T(8,128)(2,1)S(1)}, bf16[4,256,256]{2,1,0:T(8,128)(2,1)S(1)}, u32[]{:S(2)}, u32[]{:S(2)}) %collective-permute-start.34) | collective-permute-done | bytes 524320 | tf_op jit(solution)/shard_map/ppermute | solution.py:62
  234.7 3.5 while.15
  238.8 5.9 %collective-permute-start.48 = (bf16[256,256]{1,0:T(8,128)(2,1)S(1)}, bf16[256,256]{1,0:T(8,128)(2,1)S(1)}, u32[]{:S(2)}, u32[]{:S(2)}) collective-permute-start(bf16[256,256]{1,0:T(8,128)(2,1)S(1)} %get-tuple-element.166), channel_id=1, source_target_pairs={{0,1},{1,0},{2,3},{3,2},{4,5},{5,4},{6,7},{7,6},{8,9},{9,8},{10,11... | collective-permute-start | bytes 393224 | tf_op jit(solution)/shard_map/ppermute | solution.py:143
  255.9 4.9 %collective-permute-start.89 = (bf16[4,64,1536]{2,1,0:T(8,128)(2,1)}, bf16[4,64,1536]{2,1,0:T(8,128)(2,1)S(1)}, u32[]{:S(2)}, u32[]{:S(2)}) collective-permute-start(bf16[4,64,1536]{2,1,0:T(8,128)(2,1)} %collective-permute-done.87), channel_id=1, source_target_pairs={{0,32},{8,40},{16,48},{24,56},{32,64},{40,72},{48,80},{56,88},{64,... | collective-permute-start | bytes 2359304 | tf_op jit(solution)/shard_map/ppermute | solution.py:57
  266.9 3.4 collective-permute-start.58
  284.9 14.0 %collective-permute-done.90 = bf16[4,64,1536]{2,1,0:T(8,128)(2,1)S(1)} collective-permute-done((bf16[4,64,1536]{2,1,0:T(8,128)(2,1)}, bf16[4,64,1536]{2,1,0:T(8,128)(2,1)S(1)}, u32[]{:S(2)}, u32[]{:S(2)}) %collective-permute-start.90) | collective-permute-done | bytes 786464 | tf_op jit(solution)/shard_map/ppermute | solution.py:58
  300.1 3.0 collective-permute-start.67
  307.9 18.8 %collective-permute-start.92 = (bf16[2,64,1536]{2,1,0:T(8,128)(2,1)S(1)}, bf16[2,64,1536]{2,1,0:T(8,128)(2,1)S(1)}, u32[]{:S(2)}, u32[]{:S(2)}) collective-permute-start(bf16[2,64,1536]{2,1,0:T(8,128)(2,1)S(1)} %slice.158), channel_id=1, source_target_pairs={{0,224},{8,232},{16,240},{24,248},{32,0},{40,8},{48,16},{56,24},{6... | collective-permute-start | bytes 1179656 | tf_op jit(solution)/shard_map/ppermute | solution.py:63
  333.9 3.1 fusion.19
  340.1 5.0 %fusion.12 = f32[256,2048]{1,0:T(8,128)} fusion(bf16[2048,1536]{1,0:T(8,128)(2,1)} %bitcast.84, f32[256,512]{1,0:T(8,128)S(1)} %fusion.14, bf16[256,2048]{1,0:T(8,128)(2,1)S(1)} %constant_dynamic-update-slice_fusion), kind=kOutput, calls=%fused_computation.25 | convolution fusion | flops 1074528256 | bytes 7864320 | tf_op jit(solution)/shard_map/dot_general | solution.py:282
  345.0 4.8 %convolution_add_fusion = f32[256,2048]{1,0:T(8,128)S(1)} fusion(f32[256,2048]{1,0:T(8,128)} %fusion.12, bf16[2048,1536]{1,0:T(8,128)(2,1)} %bitcast.69, f32[256,512]{1,0:T(8,128)} %fusion.19, bf16[256,2048]{1,0:T(8,128)(2,1)} %copy-done.4), kind=kOutput, calls=%fused_computation.24 | convolution fusion | flops 1075052544 | bytes 9961472 | tf_op jit(solution)/shard_map/dot_general | solution.py:282
  358.0 3.7 collective-permute-done.94
  361.7 2.9 collective-permute-done.96
  367.2 3.7 gather_fusion.1
  370.9 3.7 gather_fusion
  375.2 3.3 collective-permute-start.103
  (408 shorter events, 206.5 us)
Async XLA Ops:
  0.7 21.9 %collective-permute-start = (s32[256]{0:T(256)}, s32[256]{0:T(256)S(1)}, u32[]{:S(2)}, u32[]{:S(2)}) collective-permute-start(s32[256]{0:T(256)} %param.17), channel_id=1, source_target_pairs={{0,32},{8,40},{16,48},{24,56},{32,64},{40,72},{48,80},{56,88},{64,... | collective-permute-start | bytes 3080 | tf_op jit(solution)/shard_map/ppermute | solution.py:97
  3.2 21.8 %collective-permute-start.1 = (s32[256]{0:T(256)}, s32[256]{0:T(256)S(1)}, u32[]{:S(2)}, u32[]{:S(2)}) collective-permute-start(s32[256]{0:T(256)} %param.17), channel_id=1, source_target_pairs={{0,64},{8,72},{16,80},{24,88},{32,96},{40,104},{48,112},{56,120},{... | collective-permute-start | bytes 3080 | tf_op jit(solution)/shard_map/ppermute | solution.py:97
  6.2 19.6 %collective-permute-start.2 = (s32[256]{0:T(256)}, s32[256]{0:T(256)S(1)}, u32[]{:S(2)}, u32[]{:S(2)}) collective-permute-start(s32[256]{0:T(256)} %param.17), channel_id=1, source_target_pairs={{0,96},{8,104},{16,112},{24,120},{32,128},{40,136},{48,144},{56,15... | collective-permute-start | bytes 3080 | tf_op jit(solution)/shard_map/ppermute | solution.py:97
  10.0 18.6 %collective-permute-start.3 = (s32[256]{0:T(256)}, s32[256]{0:T(256)S(1)}, u32[]{:S(2)}, u32[]{:S(2)}) collective-permute-start(s32[256]{0:T(256)} %param.17), channel_id=1, source_target_pairs={{0,128},{8,136},{16,144},{24,152},{32,160},{40,168},{48,176},{56,1... | collective-permute-start | bytes 3080 | tf_op jit(solution)/shard_map/ppermute | solution.py:97
  10.4 19.6 %collective-permute-start.4 = (s32[256]{0:T(256)}, s32[256]{0:T(256)S(1)}, u32[]{:S(2)}, u32[]{:S(2)}) collective-permute-start(s32[256]{0:T(256)} %param.17), channel_id=1, source_target_pairs={{0,160},{8,168},{16,176},{24,184},{32,192},{40,200},{48,208},{56,2... | collective-permute-start | bytes 3080 | tf_op jit(solution)/shard_map/ppermute | solution.py:97
  25.8 18.9 %collective-permute-start.10 = (bf16[256,256]{1,0:T(8,128)(2,1)S(1)}, bf16[256,256]{1,0:T(8,128)(2,1)S(1)}, u32[]{:S(2)}, u32[]{:S(2)}) collective-permute-start(bf16[256,256]{1,0:T(8,128)(2,1)S(1)} %copy-done.5), channel_id=1, source_target_pairs={{0,1},{1,0},{2,3},{3,2},{4,5},{5,4},{6,7},{7,6},{8,9},{9,8},{10,11... | collective-permute-start | bytes 393224 | tf_op jit(solution)/shard_map/ppermute | solution.py:126
  28.6 18.2 %collective-permute-start.11 = (bf16[256,256]{1,0:T(8,128)(2,1)S(1)}, bf16[256,256]{1,0:T(8,128)(2,1)S(1)}, u32[]{:S(2)}, u32[]{:S(2)}) collective-permute-start(bf16[256,256]{1,0:T(8,128)(2,1)S(1)} %copy-done.5), channel_id=1, source_target_pairs={{0,2},{1,3},{2,4},{3,5},{4,6},{5,7},{6,0},{7,1},{8,10},{9,11},{10,... | collective-permute-start | bytes 393224 | tf_op jit(solution)/shard_map/ppermute | solution.py:125
  74.5 18.3 %collective-permute-start.84 = (bf16[32,1536]{1,0:T(8,128)(2,1)}, bf16[32,1536]{1,0:T(8,128)(2,1)}, u32[]{:S(2)}, u32[]{:S(2)}) collective-permute-start(bf16[32,1536]{1,0:T(8,128)(2,1)} %slice.156), channel_id=1, source_target_pairs={{0,24},{8,0},{16,8},{24,16},{32,56},{40,32},{48,40},{56,48},{64,88... | collective-permute-start | bytes 294920 | tf_op jit(solution)/shard_map/ppermute | solution.py:63
  85.7 18.7 %collective-permute-start.71 = (bf16[64,1536]{1,0:T(8,128)(2,1)}, bf16[64,1536]{1,0:T(8,128)(2,1)}, u32[]{:S(2)}, u32[]{:S(2)}) collective-permute-start(bf16[64,1536]{1,0:T(8,128)(2,1)} %collective-permute-done.69), channel_id=1, source_target_pairs={{0,32},{8,40},{16,48},{24,56},{32,64},{40,72},{48,80},{56,88},{64,... | collective-permute-start | bytes 589832 | tf_op jit(solution)/shard_map/ppermute | solution.py:57
  85.7 23.0 %collective-permute-start.72 = (bf16[64,1536]{1,0:T(8,128)(2,1)}, bf16[64,1536]{1,0:T(8,128)(2,1)}, u32[]{:S(2)}, u32[]{:S(2)}) collective-permute-start(bf16[64,1536]{1,0:T(8,128)(2,1)} %collective-permute-done.70), channel_id=1, source_target_pairs={{0,224},{8,232},{16,240},{24,248},{32,0},{40,8},{48,16},{56,24},{6... | collective-permute-start | bytes 589832 | tf_op jit(solution)/shard_map/ppermute | solution.py:58
  92.7 17.6 %collective-permute-start.24 = (bf16[256,256]{0,1:T(8,128)(2,1)S(1)}, bf16[256,256]{0,1:T(8,128)(2,1)S(1)}, u32[]{:S(2)}, u32[]{:S(2)}) collective-permute-start(bf16[256,256]{0,1:T(8,128)(2,1)S(1)} %bitcast.192), channel_id=1, source_target_pairs={{0,32},{8,40},{16,48},{24,56},{32,64},{40,72},{48,80},{56,88},{64,... | collective-permute-start | bytes 393224 | tf_op jit(solution)/shard_map/ppermute | solution.py:57
  103.1 70.9 %collective-permute-start.85 = (bf16[4,64,1536]{2,1,0:T(8,128)(2,1)S(1)}, bf16[4,64,1536]{2,1,0:T(8,128)(2,1)}, u32[]{:S(2)}, u32[]{:S(2)}) collective-permute-start(bf16[4,64,1536]{2,1,0:T(8,128)(2,1)S(1)} %bitcast_dynamic-update-slice_fusion.41), channel_id=1, source_target_pairs={{0,32},{8,40},{16,48},{24,56},{32,64},{40,72},{48,80},{56,88},{64,... | collective-permute-start | bytes 2359304 | tf_op jit(solution)/shard_map/ppermute | solution.py:57
  104.4 101.4 %collective-permute-start.86 = (bf16[4,64,1536]{2,1,0:T(8,128)(2,1)S(1)}, bf16[4,64,1536]{2,1,0:T(8,128)(2,1)}, u32[]{:S(2)}, u32[]{:S(2)}) collective-permute-start(bf16[4,64,1536]{2,1,0:T(8,128)(2,1)S(1)} %bitcast_dynamic-update-slice_fusion.41), channel_id=1, source_target_pairs={{0,224},{8,232},{16,240},{24,248},{32,0},{40,8},{48,16},{56,24},{6... | collective-permute-start | bytes 2359304 | tf_op jit(solution)/shard_map/ppermute | solution.py:58
  113.1 18.3 %collective-permute-start.73 = (bf16[64,1536]{1,0:T(8,128)(2,1)}, bf16[64,1536]{1,0:T(8,128)(2,1)S(1)}, u32[]{:S(2)}, u32[]{:S(2)}) collective-permute-start(bf16[64,1536]{1,0:T(8,128)(2,1)} %collective-permute-done.71), channel_id=1, source_target_pairs={{0,32},{8,40},{16,48},{24,56},{32,64},{40,72},{48,80},{56,88},{64,... | collective-permute-start | bytes 589832 | tf_op jit(solution)/shard_map/ppermute | solution.py:57
  128.8 38.2 %collective-permute-start.40 = (bf16[4,256,256]{2,1,0:T(8,128)(2,1)}, bf16[4,256,256]{2,1,0:T(8,128)(2,1)}, u32[]{:S(2)}, u32[]{:S(2)}) collective-permute-start(bf16[4,256,256]{2,1,0:T(8,128)(2,1)} %bitcast_dynamic-update-slice_fusion.45), channel_id=1, source_target_pairs={{0,32},{8,40},{16,48},{24,56},{32,64},{40,72},{48,80},{56,88},{64,... | collective-permute-start | bytes 1572872 | tf_op jit(solution)/shard_map/ppermute | solution.py:57
  166.5 21.0 %collective-permute-start.32 = (bf16[8,256,256]{2,1,0:T(8,128)(2,1)S(1)}, bf16[8,256,256]{2,1,0:T(8,128)(2,1)S(1)}, u32[]{:S(2)}, u32[]{:S(2)}) collective-permute-start(bf16[8,256,256]{2,1,0:T(8,128)(2,1)S(1)} %constant_dynamic-update-slice_fusion.8), channel_id=1, source_target_pairs={{0,8},{8,16},{16,24},{24,0},{32,40},{40,48},{48,56},{56,32},{64,72... | collective-permute-start | bytes 3145736 | tf_op jit(solution)/shard_map/ppermute | solution.py:57
  167.0 20.7 %collective-permute-start.33 = (bf16[8,256,256]{2,1,0:T(8,128)(2,1)S(1)}, bf16[8,256,256]{2,1,0:T(8,128)(2,1)S(1)}, u32[]{:S(2)}, u32[]{:S(2)}) collective-permute-start(bf16[8,256,256]{2,1,0:T(8,128)(2,1)S(1)} %constant_dynamic-update-slice_fusion.8), channel_id=1, source_target_pairs={{0,24},{8,0},{16,8},{24,16},{32,56},{40,32},{48,40},{56,48},{64,88... | collective-permute-start | bytes 3145736 | tf_op jit(solution)/shard_map/ppermute | solution.py:58
  181.4 82.7 %collective-permute-start.77 = (bf16[8,64,1536]{2,1,0:T(8,128)(2,1)}, bf16[8,64,1536]{2,1,0:T(8,128)(2,1)}, u32[]{:S(2)}, u32[]{:S(2)}) collective-permute-start(bf16[8,64,1536]{2,1,0:T(8,128)(2,1)} %bitcast_dynamic-update-slice_fusion.43), channel_id=1, source_target_pairs={{0,8},{8,16},{16,24},{24,0},{32,40},{40,48},{48,56},{56,32},{64,72... | collective-permute-start | bytes 4718600 | tf_op jit(solution)/shard_map/ppermute | solution.py:57
  187.8 44.6 %collective-permute-start.34 = (bf16[4,256,256]{2,1,0:T(8,128)(2,1)S(1)}, bf16[4,256,256]{2,1,0:T(8,128)(2,1)S(1)}, u32[]{:S(2)}, u32[]{:S(2)}) collective-permute-start(bf16[4,256,256]{2,1,0:T(8,128)(2,1)S(1)} %slice.140), channel_id=1, source_target_pairs={{0,8},{8,16},{16,24},{24,0},{32,40},{40,48},{48,56},{56,32},{64,72... | collective-permute-start | bytes 1572872 | tf_op jit(solution)/shard_map/ppermute | solution.py:62
  202.6 30.1 %collective-permute-start.35 = (bf16[4,256,256]{2,1,0:T(8,128)(2,1)S(1)}, bf16[4,256,256]{2,1,0:T(8,128)(2,1)S(1)}, u32[]{:S(2)}, u32[]{:S(2)}) collective-permute-start(bf16[4,256,256]{2,1,0:T(8,128)(2,1)S(1)} %slice.141), channel_id=1, source_target_pairs={{0,24},{8,0},{16,8},{24,16},{32,56},{40,32},{48,40},{56,48},{64,88... | collective-permute-start | bytes 1572872 | tf_op jit(solution)/shard_map/ppermute | solution.py:63
  205.0 61.8 %collective-permute-start.78 = (bf16[8,64,1536]{2,1,0:T(8,128)(2,1)}, bf16[8,64,1536]{2,1,0:T(8,128)(2,1)}, u32[]{:S(2)}, u32[]{:S(2)}) collective-permute-start(bf16[8,64,1536]{2,1,0:T(8,128)(2,1)} %bitcast_dynamic-update-slice_fusion.43), channel_id=1, source_target_pairs={{0,24},{8,0},{16,8},{24,16},{32,56},{40,32},{48,40},{56,48},{64,88... | collective-permute-start | bytes 4718600 | tf_op jit(solution)/shard_map/ppermute | solution.py:58
  205.8 41.0 %collective-permute-start.87 = (bf16[4,64,1536]{2,1,0:T(8,128)(2,1)}, bf16[4,64,1536]{2,1,0:T(8,128)(2,1)}, u32[]{:S(2)}, u32[]{:S(2)}) collective-permute-start(bf16[4,64,1536]{2,1,0:T(8,128)(2,1)} %collective-permute-done.85), channel_id=1, source_target_pairs={{0,32},{8,40},{16,48},{24,56},{32,64},{40,72},{48,80},{56,88},{64,... | collective-permute-start | bytes 2359304 | tf_op jit(solution)/shard_map/ppermute | solution.py:57
  232.4 17.6 %collective-permute-start.88 = (bf16[4,64,1536]{2,1,0:T(8,128)(2,1)}, bf16[4,64,1536]{2,1,0:T(8,128)(2,1)}, u32[]{:S(2)}, u32[]{:S(2)}) collective-permute-start(bf16[4,64,1536]{2,1,0:T(8,128)(2,1)} %collective-permute-done.86), channel_id=1, source_target_pairs={{0,224},{8,232},{16,240},{24,248},{32,0},{40,8},{48,16},{56,24},{6... | collective-permute-start | bytes 2359304 | tf_op jit(solution)/shard_map/ppermute | solution.py:58
  255.9 27.4 %collective-permute-start.89 = (bf16[4,64,1536]{2,1,0:T(8,128)(2,1)}, bf16[4,64,1536]{2,1,0:T(8,128)(2,1)S(1)}, u32[]{:S(2)}, u32[]{:S(2)}) collective-permute-start(bf16[4,64,1536]{2,1,0:T(8,128)(2,1)} %collective-permute-done.87), channel_id=1, source_target_pairs={{0,32},{8,40},{16,48},{24,56},{32,64},{40,72},{48,80},{56,88},{64,... | collective-permute-start | bytes 2359304 | tf_op jit(solution)/shard_map/ppermute | solution.py:57
  279.2 19.8 %collective-permute-start.90 = (bf16[4,64,1536]{2,1,0:T(8,128)(2,1)}, bf16[4,64,1536]{2,1,0:T(8,128)(2,1)S(1)}, u32[]{:S(2)}, u32[]{:S(2)}) collective-permute-start(bf16[4,64,1536]{2,1,0:T(8,128)(2,1)} %collective-permute-done.88), channel_id=1, source_target_pairs={{0,224},{8,232},{16,240},{24,248},{32,0},{40,8},{48,16},{56,24},{6... | collective-permute-start | bytes 2359304 | tf_op jit(solution)/shard_map/ppermute | solution.py:58
  279.3 49.3 %collective-permute-start.79 = (bf16[4,64,1536]{2,1,0:T(8,128)(2,1)S(1)}, bf16[4,64,1536]{2,1,0:T(8,128)(2,1)S(1)}, u32[]{:S(2)}, u32[]{:S(2)}) collective-permute-start(bf16[4,64,1536]{2,1,0:T(8,128)(2,1)S(1)} %slice.150), channel_id=1, source_target_pairs={{0,8},{8,16},{16,24},{24,0},{32,40},{40,48},{48,56},{56,32},{64,72... | collective-permute-start | bytes 2359304 | tf_op jit(solution)/shard_map/ppermute | solution.py:62
  279.4 50.2 %collective-permute-start.80 = (bf16[4,64,1536]{2,1,0:T(8,128)(2,1)S(1)}, bf16[4,64,1536]{2,1,0:T(8,128)(2,1)S(1)}, u32[]{:S(2)}, u32[]{:S(2)}) collective-permute-start(bf16[4,64,1536]{2,1,0:T(8,128)(2,1)S(1)} %slice.151), channel_id=1, source_target_pairs={{0,24},{8,0},{16,8},{24,16},{32,56},{40,32},{48,40},{56,48},{64,88... | collective-permute-start | bytes 2359304 | tf_op jit(solution)/shard_map/ppermute | solution.py:63
  282.3 17.8 %collective-permute-start.62 = (bf16[256,256]{1,0:T(8,128)(2,1)S(1)}, bf16[256,256]{1,0:T(8,128)(2,1)S(1)}, u32[]{:S(2)}, u32[]{:S(2)}) collective-permute-start(bf16[256,256]{1,0:T(8,128)(2,1)S(1)} %get-tuple-element.149), channel_id=1, source_target_pairs={{0,1},{1,0},{2,3},{3,2},{4,5},{5,4},{6,7},{7,6},{8,9},{9,8},{10,11... | collective-permute-start | bytes 393224 | tf_op jit(solution)/shard_map/ppermute | solution.py:126
  283.3 19.8 %collective-permute-start.63 = (bf16[256,256]{1,0:T(8,128)(2,1)S(1)}, bf16[256,256]{1,0:T(8,128)(2,1)S(1)}, u32[]{:S(2)}, u32[]{:S(2)}) collective-permute-start(bf16[256,256]{1,0:T(8,128)(2,1)S(1)} %get-tuple-element.149), channel_id=1, source_target_pairs={{0,2},{1,3},{2,4},{3,5},{4,6},{5,7},{6,0},{7,1},{8,10},{9,11},{10,... | collective-permute-start | bytes 393224 | tf_op jit(solution)/shard_map/ppermute | solution.py:125
  304.8 28.3 %collective-permute-start.91 = (bf16[2,64,1536]{2,1,0:T(8,128)(2,1)S(1)}, bf16[2,64,1536]{2,1,0:T(8,128)(2,1)S(1)}, u32[]{:S(2)}, u32[]{:S(2)}) collective-permute-start(bf16[2,64,1536]{2,1,0:T(8,128)(2,1)S(1)} %slice.157), channel_id=1, source_target_pairs={{0,32},{8,40},{16,48},{24,56},{32,64},{40,72},{48,80},{56,88},{64,... | collective-permute-start | bytes 1179656 | tf_op jit(solution)/shard_map/ppermute | solution.py:62
  306.2 20.6 %collective-permute-start.66 = (bf16[256,256]{1,0:T(8,128)(2,1)S(1)}, bf16[256,256]{1,0:T(8,128)(2,1)S(1)}, u32[]{:S(2)}, u32[]{:S(2)}) collective-permute-start(bf16[256,256]{1,0:T(8,128)(2,1)S(1)} %collective-permute-done.65), channel_id=1, source_target_pairs={{0,1},{1,0},{2,3},{3,2},{4,5},{5,4},{6,7},{7,6},{8,9},{9,8},{10,11... | collective-permute-start | bytes 393224 | tf_op jit(solution)/shard_map/ppermute | solution.py:126
  307.9 29.0 %collective-permute-start.92 = (bf16[2,64,1536]{2,1,0:T(8,128)(2,1)S(1)}, bf16[2,64,1536]{2,1,0:T(8,128)(2,1)S(1)}, u32[]{:S(2)}, u32[]{:S(2)}) collective-permute-start(bf16[2,64,1536]{2,1,0:T(8,128)(2,1)S(1)} %slice.158), channel_id=1, source_target_pairs={{0,224},{8,232},{16,240},{24,248},{32,0},{40,8},{48,16},{56,24},{6... | collective-permute-start | bytes 1179656 | tf_op jit(solution)/shard_map/ppermute | solution.py:63
  (94 other events, 1146.8 us)

commit v2 on v1

--- a/solution.py
+++ b/solution.py
@@ -88,45 +88,37 @@
     return whole.reshape(RINGS * rows, cols)
 
 
-def gather_ids(segment_ids):
-    rows = segment_ids.shape[0]
-    own_z = ring_place(ZS, XS)
-    own_x = ring_place(XS, 1)
-    line = jnp.zeros((ZS, rows), jnp.int32)
-    for step in range(ZS):
-        part = lax.ppermute(segment_ids, "req", ring_shift(ZS, XS, step)) if step else segment_ids
-        line = lax.dynamic_update_slice(line, part[None], ((own_z - step) % ZS, 0))
-    whole = jnp.zeros((ZS, XS, rows), jnp.int32)
-    for step in range(XS):
-        part = lax.ppermute(line, "req", ring_shift(XS, 1, step)) if step else line
-        whole = lax.dynamic_update_slice(whole, part[:, None], (0, (own_x - step) % XS, 0))
-    return whole.reshape(-1)
-
-
 def mlp_pairs(dy, dc):
     return [(m, ((m // 2 + dy) % YS) * 2 + (m % 2 ^ dc)) for m in range(2 * YS)]
 
 
+def exchange_sum(values, axis, size):
+    bit = 1
+    while bit < size:
+        values = values + lax.ppermute(values, axis, [(m, m ^ bit) for m in range(size)])
+        bit *= 2
+    return values
+
+
 def mlp_sum(values):
-    total = values
-    for dy in range(YS):
-        for dc in range(2):
-            if dy or dc:
-                total = total + lax.ppermute(values, "mlp", mlp_pairs(dy, dc))
-    return total
-
-
-def mlp_gather(piece):
-    rows, width = piece.shape
+    return exchange_sum(values, "mlp", 2 * YS)
+
+
+def mlp_gather(piece, axis):
+    width = piece.shape[axis]
     own = lax.axis_index("mlp")
     own_y, own_c = own // 2, own % 2
-    whole = jnp.zeros((rows, width * 2 * YS), piece.dtype)
+    shape = list(piece.shape)
+    shape[axis] = width * 2 * YS
+    whole = jnp.zeros(shape, piece.dtype)
     for dy in range(YS):
         part = lax.ppermute(piece, "mlp", mlp_pairs(dy, 0)) if dy else piece
         other = lax.ppermute(part, "mlp", mlp_pairs(0, 1))
         src_y = (own_y - dy) % YS
-        whole = lax.dynamic_update_slice(whole, part, (0, (src_y * 2 + own_c) * width))
-        whole = lax.dynamic_update_slice(whole, other, (0, (src_y * 2 + 1 - own_c) * width))
+        place = (src_y * 2 + own_c) * width
+        whole = lax.dynamic_update_slice_in_dim(whole, part, place, axis)
+        place = (src_y * 2 + 1 - own_c) * width
+        whole = lax.dynamic_update_slice_in_dim(whole, other, place, axis)
     return whole
 
 
@@ -176,31 +168,36 @@
     model_width = query_weight.shape[0]
     head_dim = HD
     head_count = local_width // head_dim
-    half_units = gate_weight.shape[1] // 2
-    ffn_low = gather_req(
-        jnp.concatenate([w[:, :half_units] for w in (gate_weight, up_weight, down_weight)], axis=1),
-        True,
-    )
-    ffn_high = gather_req(
-        jnp.concatenate([w[:, half_units:] for w in (gate_weight, up_weight, down_weight)], axis=1),
-        False,
-    )
-    seg_part = gather_ids(segment_ids)
-    full_rows = mlp_gather(tokens)
+    seg_total = lax.axis_size("req") // 2 + 1
+    seg_range = jnp.arange(seg_total, dtype=jnp.int32)
+    matches = segment_ids[:, None] == seg_range[None, :]
+    counts = jnp.sum(matches.astype(jnp.int32), axis=0)
+    totals = exchange_sum(counts, "req", RINGS)
+    units = gate_weight.shape[1]
+    gate_up = lax.all_gather(
+        jnp.concatenate([gate_weight, up_weight], axis=1), "req", axis=0, tiled=True
+    )
+    full_rows = mlp_gather(tokens, 1)
     query_proj = jnp.dot(full_rows, query_weight, preferred_element_type=jnp.float32)
     key_proj = jnp.dot(full_rows, key_weight, preferred_element_type=jnp.float32)
     value_proj = jnp.dot(full_rows, value_weight, preferred_element_type=jnp.float32)
-    query_total, key_total = mlp_sum(
-        jnp.stack([jnp.sum(query_proj * query_proj, axis=1), jnp.sum(key_proj * key_proj, axis=1)])
-    )
+    gain_row = jnp.arange(2 * YS, dtype=jnp.int32)[:, None] == lax.axis_index("mlp")
+    shared = mlp_sum(
+        jnp.concatenate(
+            [
+                jnp.sum(query_proj * query_proj, axis=1)[None],
+                jnp.sum(key_proj * key_proj, axis=1)[None],
+                jnp.where(gain_row, attention_gain[None, :], 0.0),
+            ]
+        )
+    )
+    query_total, key_total = shared[0], shared[1]
+    full_gain = shared[2:].reshape(-1)
     query_n = (
         query_proj * lax.rsqrt(query_total / model_width + norm_eps)[:, None] * query_gain[None, :]
     )
     key_n = key_proj * lax.rsqrt(key_total / model_width + norm_eps)[:, None] * key_gain[None, :]
-    seg_total = lax.axis_size("req") // 2 + 1
-    seg_range = jnp.arange(seg_total, dtype=jnp.int32)
-    matches = segment_ids[:, None] == seg_range[None, :]
-    seg_starts = jnp.sum((seg_part[:, None] < seg_range[None, :]).astype(jnp.int32), axis=0)
+    seg_starts = jnp.cumsum(totals) - totals
     row_base = lax.axis_index("req") * tok_rows
     global_index = row_base + jnp.arange(tok_rows, dtype=jnp.int32)
     own_start = jnp.sum(jnp.where(matches, seg_starts[None, :], 0), axis=1)
@@ -209,6 +206,8 @@
     query_r = rotate(query_n, cosine_table, sine_table, head_dim).astype(jnp.bfloat16)
     key_r = rotate(key_n, cosine_table, sine_table, head_dim).astype(jnp.bfloat16)
     value_b = value_proj.astype(jnp.bfloat16)
+    out_rows, _ = lax.optimization_barrier((out_weight, query_total))
+    out_full = mlp_gather(out_rows, 0)
     query_heads = query_r.reshape(tok_rows, head_count, head_dim)
     score_scale = head_dim ** (-0.5)
     pages_here = page_source.shape[0]
@@ -218,8 +217,13 @@
         jnp.zeros((head_count, tok_rows), jnp.float32),
         jnp.zeros((tok_rows, head_count, head_dim), jnp.float32),
     )
-    fetched = (gather_req(key_r, True), gather_req(value_b, False))
-    key_part, value_part = fetched
+    key_part, value_part = gather_req(key_r, True), gather_req(value_b, False)
+    key_part, value_part, down_weight = lax.optimization_barrier(
+        (key_part, value_part, down_weight)
+    )
+    half_units = units // 2
+    down_low = gather_req(down_weight[:, :half_units], True)
+    down_high = gather_req(down_weight[:, half_units:], False)
     row_count = key_part.shape[0]
     block_rows = 512
 
@@ -232,12 +236,10 @@
         value_block = lax.dynamic_slice_in_dim(value_part, offset, block_rows, 0).reshape(
             block_rows, head_count, head_dim
         )
-        seg_block = lax.dynamic_slice_in_dim(seg_part, offset, block_rows, 0)
         key_index = offset + jnp.arange(block_rows, dtype=jnp.int32)
         visible = (
-            (segment_ids[:, None] == seg_block[None, :])
+            (own_start[:, None] <= key_index[None, :])
             & (global_index[:, None] >= key_index[None, :])
-            & (key_index[None, :] >= 0)
         )
         scores = (
             jnp.einsum("thd,rhd->htr", query_heads, key_block, preferred_element_type=jnp.float32)
@@ -264,25 +266,26 @@
     page_cache = jnp.stack([key_part[page_rows], value_part[page_rows]], axis=1)
     run_max, run_sum, run_out = attn_state
     attended = (run_out / run_sum.T[:, :, None]).reshape(tok_rows, local_width).astype(jnp.bfloat16)
-    projected = jnp.dot(attended, out_weight, preferred_element_type=jnp.float32)
-    residual = (
-        tokens.astype(jnp.float32) + post_norm(projected, attention_gain, model_width)
+    projected = jnp.dot(
+        mlp_gather(attended, 1), out_full, preferred_element_type=jnp.float32
+    )
+    mean_square = jnp.sum(projected * projected, axis=1) / model_width
+    normed = (
+        full_rows.astype(jnp.float32)
+        + projected * lax.rsqrt(mean_square + norm_eps)[:, None] * full_gain[None, :]
     ).astype(jnp.bfloat16)
-    normed = mlp_gather(residual)
+    residual = lax.dynamic_slice_in_dim(
+        normed, lax.axis_index("mlp") * local_width, local_width, 1
+    )
     contract = (((1,), (1,)), ((), ()))
-    down_act = None
-    for part in (ffn_low, ffn_high):
-        gate_act = jnp.dot(
-            normed, part[:, :half_units], preferred_element_type=jnp.float32
-        )
-        up_act = jnp.dot(
-            normed, part[:, half_units : 2 * half_units], preferred_element_type=jnp.float32
-        )
-        hidden = (jax.nn.silu(gate_act) * up_act).astype(jnp.bfloat16)
-        down = lax.dot_general(
-            hidden, part[:, 2 * half_units :], contract, preferred_element_type=jnp.float32
-        )
-        down_act = down if down_act is None else down_act + down
+    gate_act = jnp.dot(normed, gate_up[:, :units], preferred_element_type=jnp.float32)
+    up_act = jnp.dot(normed, gate_up[:, units:], preferred_element_type=jnp.float32)
+    hidden = (jax.nn.silu(gate_act) * up_act).astype(jnp.bfloat16)
+    down_act = lax.dot_general(
+        hidden[:, :half_units], down_low, contract, preferred_element_type=jnp.float32
+    ) + lax.dot_general(
+        hidden[:, half_units:], down_high, contract, preferred_element_type=jnp.float32
+    )
     layer_out = (
         residual.astype(jnp.float32) + post_norm(down_act, feedforward_gain, model_width)
     ).astype(jnp.bfloat16)

time: 391 us -> 414 us (1.059)
  the two profiles are of different devices: /device:TPU:1 before, /device:TPU:96 now
where the time goes in v2:
time: 414 us; the launch traced here: 406 us
  waiting for transfers between devices  157 us (38%)
  starting transfers between devices  111 us (27%)
  local copies, waits for them, and re-layouts  72.6 us (18%)
  other arithmetic  25 us (6%)
  matrix products  21.6 us (5%)
  between operations  18.3 us (4%)
    ppermute x16, waiting for transfers between devices, ring_gather(): ahead = lax.ppermute(ahead, 'req', ring_shift(size, stride, 1))  38.6 us
    ppermute x16, starting transfers between devices, ring_gather(): ahead = lax.ppermute(ahead, 'req', ring_shift(size, stride, 1))  34.4 us
    ppermute x11, waiting for transfers between devices, exchange_sum(): lax.ppermute(values, axis, [(m, m ^ bit) for m in range(size)])  32.4 us
    ppermute x9, waiting for transfers between devices, mlp_gather(): part = lax.ppermute(piece, 'mlp', mlp_pairs(dy, 0)) if dy else piece  27.2 us
    ppermute x8, waiting for transfers between devices, ring_gather(): behind = lax.ppermute(behind[half:], 'req', ring_shift(size, stride, -1))  21.6 us
    ppermute x16, waiting for transfers between devices, ring_gather(): behind = lax.ppermute(behind, 'req', ring_shift(size, stride, -1))  20.6 us
    ppermute x9, starting transfers between devices, mlp_gather(): part = lax.ppermute(piece, 'mlp', mlp_pairs(dy, 0)) if dy else piece  16.6 us
    dynamic_update_slice x18, local copies, waits for them, and re-layouts, put_z(): return lax.dynamic_update_slice(state, part[None], (place, row, 0, 0))  15.8 us
  transfers between devices with their start and end apart: 88, of which 37 were waited for; matrix products, arithmetic and copies ran while one was open for 26% of the time, Pallas kernels for 0%

profile of v2, /device:TPU:96, one launch (start us, length us, event | category | flops | bytes accessed | tf_op | source)
XLA Modules:
  0.0 406.0 jit_solution(11976334143132950218)
XLA Ops:
  19.6 4.4 %broadcast_in_dim.316 = bf16[2048,2048]{1,0:T(8,128)(2,1)} broadcast(bf16[]{:T(256)} %constant.319.clone.1), dimensions={} | broadcast | bytes 8388610 | tf_op jit(solution)/shard_map/broadcast_in_dim | solution.py:113
  34.2 3.7 collective-permute-done.9
  39.0 4.7 %collective-permute-done.10 = s32[17]{0:T(128)} collective-permute-done((s32[17]{0:T(128)}, s32[17]{0:T(128)}, u32[]{:S(2)}, u32[]{:S(2)}) %collective-permute-start.10) | collective-permute-done | bytes 100 | tf_op jit(solution)/shard_map/ppermute | solution.py:98
  44.9 4.5 %collective-permute-start.11 = (s32[17]{0:T(128)}, s32[17]{0:T(128)}, u32[]{:S(2)}, u32[]{:S(2)}) collective-permute-start(s32[17]{0:T(128)} %add.563), channel_id=1, source_target_pairs={{0,128},{8,136},{16,144},{24,152},{32,160},{40,168},{48,176},{56,1... | collective-permute-start | bytes 212 | tf_op jit(solution)/shard_map/ppermute | solution.py:98
  69.2 14.4 %collective-permute-done.13 = f32[10,256]{1,0:T(8,128)S(1)} collective-permute-done((f32[10,256]{1,0:T(8,128)S(1)}, f32[10,256]{1,0:T(8,128)S(1)}, u32[]{:S(2)}, u32[]{:S(2)}) %collective-permute-start.13) | collective-permute-done | bytes 10272 | tf_op jit(solution)/shard_map/ppermute | solution.py:98
  101.1 4.0 collective-permute-done.16
  120.1 11.2 %collective-permute-done.19 = bf16[256,256]{0,1:T(8,128)(2,1)S(1)} collective-permute-done((bf16[256,256]{0,1:T(8,128)(2,1)S(1)}, bf16[256,256]{0,1:T(8,128)(2,1)S(1)}, u32[]{:S(2)}, u32[]{:S(2)}) %collective-permute-start.19) | collective-permute-done | bytes 131104 | tf_op jit(solution)/shard_map/ppermute | solution.py:57
  138.4 8.4 %collective-permute-done.22 = bf16[128,256]{0,1:T(8,128)(2,1)S(1)} collective-permute-done((bf16[128,256]{0,1:T(8,128)(2,1)S(1)}, bf16[128,256]{0,1:T(8,128)(2,1)S(1)}, u32[]{:S(2)}, u32[]{:S(2)}) %collective-permute-start.22) | collective-permute-done | bytes 65568 | tf_op jit(solution)/shard_map/ppermute | solution.py:63
  156.9 3.2 collective-permute-start.24
  167.1 4.6 %collective-permute-done.49 = bf16[256,2048]{1,0:T(8,128)(2,1)} collective-permute-done((bf16[256,2048]{1,0:T(8,128)(2,1)}, bf16[256,2048]{1,0:T(8,128)(2,1)}, u32[]{:S(2)}, u32[]{:S(2)}) %collective-permute-start.49) | collective-permute-done | bytes 1048608 | tf_op jit(solution)/shard_map/ppermute | solution.py:115
  171.7 22.6 %collective-permute-done.51 = bf16[256,2048]{1,0:T(8,128)(2,1)S(1)} collective-permute-done((bf16[256,2048]{1,0:T(8,128)(2,1)}, bf16[256,2048]{1,0:T(8,128)(2,1)S(1)}, u32[]{:S(2)}, u32[]{:S(2)}) %collective-permute-start.51) | collective-permute-done | bytes 1048608 | tf_op jit(solution)/shard_map/ppermute | solution.py:115
  198.1 11.5 %collective-permute-done.35 = bf16[4,256,256]{2,1,0:T(8,128)(2,1)S(1)} collective-permute-done((bf16[4,256,256]{2,1,0:T(8,128)(2,1)S(1)}, bf16[4,256,256]{2,1,0:T(8,128)(2,1)S(1)}, u32[]{:S(2)}, u32[]{:S(2)}) %collective-permute-start.35) | collective-permute-done | bytes 524320 | tf_op jit(solution)/shard_map/ppermute | solution.py:57
  214.6 3.2 collective-permute-start.37
  225.6 3.7 collective-permute-done.38
  232.3 16.6 %while.15 = (s32[]{:T(128)}, f32[2,256]{1,0:T(2,128)S(1)}, f32[2,256]{1,0:T(2,128)S(1)}, f32[256,2,128]{0,2,1:T(8,128)S(1)}, s32[]{:T(128)}, /*index=5*/s32[256]...) while((s32[]{:T(128)}, f32[2,256]{1,0:T(2,128)S(1)}, ...), condition=%wide.region_8.9_spmd.clone, body=%wide.region_5.8_spmd.clone.sunk | while | flops 137103616 | bytes 6986943 | solution.py:264
  254.8 5.8 %collective-permute-done.65 = bf16[64,512]{1,0:T(8,128)(2,1)S(1)} collective-permute-done((bf16[64,512]{1,0:T(8,128)(2,1)S(1)}, bf16[64,512]{1,0:T(8,128)(2,1)S(1)}, u32[]{:S(2)}, u32[]{:S(2)}) %collective-permute-start.65) | collective-permute-done | bytes 65568 | tf_op jit(solution)/shard_map/ppermute | solution.py:57
  264.9 5.1 %collective-permute-done.67 = bf16[32,512]{1,0:T(8,128)(2,1)S(1)} collective-permute-done((bf16[32,512]{1,0:T(8,128)(2,1)S(1)}, bf16[32,512]{1,0:T(8,128)(2,1)S(1)}, u32[]{:S(2)}, u32[]{:S(2)}) %collective-permute-start.67) | collective-permute-done | bytes 32800 | tf_op jit(solution)/shard_map/ppermute | solution.py:62
  273.9 8.2 %collective-permute-start.55 = (bf16[64,512]{1,0:T(8,128)(2,1)S(1)}, bf16[64,512]{1,0:T(8,128)(2,1)S(1)}, u32[]{:S(2)}, u32[]{:S(2)}) collective-permute-start(bf16[64,512]{1,0:T(8,128)(2,1)S(1)} %collective-permute-done.53), channel_id=1, source_target_pairs={{0,32},{8,40},{16,48},{24,56},{32,64},{40,72},{48,80},{56,88},{64,... | collective-permute-start | bytes 196616 | tf_op jit(solution)/shard_map/ppermute | solution.py:57
  284.4 6.6 %collective-permute-done.56 = bf16[64,512]{1,0:T(8,128)(2,1)S(1)} collective-permute-done((bf16[64,512]{1,0:T(8,128)(2,1)S(1)}, bf16[64,512]{1,0:T(8,128)(2,1)S(1)}, u32[]{:S(2)}, u32[]{:S(2)}) %collective-permute-start.56) | collective-permute-done | bytes 65568 | tf_op jit(solution)/shard_map/ppermute | solution.py:58
  294.2 3.3 collective-permute-start.57
  299.4 5.8 %collective-permute-done.58 = bf16[64,512]{1,0:T(8,128)(2,1)S(1)} collective-permute-done((bf16[64,512]{1,0:T(8,128)(2,1)S(1)}, bf16[64,512]{1,0:T(8,128)(2,1)S(1)}, u32[]{:S(2)}, u32[]{:S(2)}) %collective-permute-start.58) | collective-permute-done | bytes 65568 | tf_op jit(solution)/shard_map/ppermute | solution.py:58
  309.8 4.5 %collective-permute-done.60 = bf16[32,512]{1,0:T(8,128)(2,1)S(1)} collective-permute-done((bf16[32,512]{1,0:T(8,128)(2,1)S(1)}, bf16[32,512]{1,0:T(8,128)(2,1)S(1)}, u32[]{:S(2)}, u32[]{:S(2)}) %collective-permute-start.60) | collective-permute-done | bytes 32800 | tf_op jit(solution)/shard_map/ppermute | solution.py:63
  316.9 3.3 collective-permute-start.62
  320.3 5.9 %multiply_reduce_fusion = (f32[256]{0:T(256)S(1)}, f32[256,2048]{1,0:T(8,128)S(1)}) fusion(bf16[256,2048]{1,0:T(8,128)(2,1)S(1)} %constant_dynamic-update-slice_fusion.8, bf16[2048,2048]{1,0:T(8,128)(2,1)} %constant_dynamic-update-slice_fusion), kind=kOutput, calls=%fused_computation.29 | convolution fusion | flops 2148531968 | bytes 11535360 | tf_op jit(solution)/shard_map/dot_general | solution.py:269
  330.1 4.7 %collective-permute-done.71 = bf16[4,64,512]{2,1,0:T(8,128)(2,1)S(1)} collective-permute-done((bf16[4,64,512]{2,1,0:T(8,128)(2,1)S(1)}, bf16[4,64,512]{2,1,0:T(8,128)(2,1)S(1)}, u32[]{:S(2)}, u32[]{:S(2)}) %collective-permute-start.71) | collective-permute-done | bytes 262176 | tf_op jit(solution)/shard_map/ppermute | solution.py:57
  334.8 3.2 collective-permute-start.73
  339.8 3.3 collective-permute-start.64
  344.8 3.3 collective-permute-start.75
  356.5 3.6 fusion.14
  376.2 3.5 collective-permute-done.78
  385.3 3.7 gather_fusion
  389.0 3.7 gather_fusion.1
  (410 shorter events, 205.7 us)
Async XLA Ops:
  7.2 349.3 %all-gather.2.cloned.1.call-start = ((), (), s32[]{:S(2)}) async-start(), calls=%async_computation | async-start | bytes 8650752 | tf_op jit(solution)/shard_map/all_gather | solution.py:177
  7.2 52.1 %collective-permute-start = (bf16[256,256]{1,0:T(8,128)(2,1)}, bf16[256,256]{1,0:T(8,128)(2,1)S(1)}, u32[]{:S(2)}, u32[]{:S(2)}) collective-permute-start(bf16[256,256]{1,0:T(8,128)(2,1)} %param.16), channel_id=1, source_target_pairs={{0,1},{1,0},{2,3},{3,2},{4,5},{5,4},{6,7},{7,6},{8,9},{9,8},{10,11... | collective-permute-start | bytes 393224 | tf_op jit(solution)/shard_map/ppermute | solution.py:116
  7.3 52.7 %collective-permute-start.1 = (bf16[256,256]{1,0:T(8,128)(2,1)}, bf16[256,256]{1,0:T(8,128)(2,1)}, u32[]{:S(2)}, u32[]{:S(2)}) collective-permute-start(bf16[256,256]{1,0:T(8,128)(2,1)} %param.16), channel_id=1, source_target_pairs={{0,2},{1,3},{2,4},{3,5},{4,6},{5,7},{6,0},{7,1},{8,10},{9,11},{10,... | collective-permute-start | bytes 393224 | tf_op jit(solution)/shard_map/ppermute | solution.py:115
  9.0 51.2 %collective-permute-start.3 = (bf16[256,256]{1,0:T(8,128)(2,1)}, bf16[256,256]{1,0:T(8,128)(2,1)S(1)}, u32[]{:S(2)}, u32[]{:S(2)}) collective-permute-start(bf16[256,256]{1,0:T(8,128)(2,1)} %param.16), channel_id=1, source_target_pairs={{0,4},{1,5},{2,6},{3,7},{4,0},{5,1},{6,2},{7,3},{8,12},{9,13},{10,... | collective-permute-start | bytes 393224 | tf_op jit(solution)/shard_map/ppermute | solution.py:115
  11.9 48.6 %collective-permute-start.5 = (bf16[256,256]{1,0:T(8,128)(2,1)}, bf16[256,256]{1,0:T(8,128)(2,1)S(1)}, u32[]{:S(2)}, u32[]{:S(2)}) collective-permute-start(bf16[256,256]{1,0:T(8,128)(2,1)} %param.16), channel_id=1, source_target_pairs={{0,6},{1,7},{2,0},{3,1},{4,2},{5,3},{6,4},{7,5},{8,14},{9,15},{10,... | collective-permute-start | bytes 393224 | tf_op jit(solution)/shard_map/ppermute | solution.py:115
  52.6 102.4 %collective-permute-start.46 = (bf16[256,2048]{1,0:T(8,128)(2,1)}, bf16[256,2048]{1,0:T(8,128)(2,1)}, u32[]{:S(2)}, u32[]{:S(2)}) collective-permute-start(bf16[256,2048]{1,0:T(8,128)(2,1)} %param.22), channel_id=1, source_target_pairs={{0,1},{1,0},{2,3},{3,2},{4,5},{5,4},{6,7},{7,6},{8,9},{9,8},{10,11... | collective-permute-start | bytes 3145736 | tf_op jit(solution)/shard_map/ppermute | solution.py:116
  59.3 97.6 %collective-permute-start.47 = (bf16[256,2048]{1,0:T(8,128)(2,1)}, bf16[256,2048]{1,0:T(8,128)(2,1)}, u32[]{:S(2)}, u32[]{:S(2)}) collective-permute-start(bf16[256,2048]{1,0:T(8,128)(2,1)} %param.22), channel_id=1, source_target_pairs={{0,2},{1,3},{2,4},{3,5},{4,6},{5,7},{6,0},{7,1},{8,10},{9,11},{10,... | collective-permute-start | bytes 3145736 | tf_op jit(solution)/shard_map/ppermute | solution.py:115
  64.3 19.3 %collective-permute-start.13 = (f32[10,256]{1,0:T(8,128)S(1)}, f32[10,256]{1,0:T(8,128)S(1)}, u32[]{:S(2)}, u32[]{:S(2)}) collective-permute-start(f32[10,256]{1,0:T(8,128)S(1)} %fusion.23), channel_id=1, source_target_pairs={{0,2},{1,3},{2,0},{3,1},{4,6},{5,7},{6,4},{7,5},{8,10},{9,11},{10,... | collective-permute-start | bytes 30728 | tf_op jit(solution)/shard_map/ppermute | solution.py:98
  109.2 40.7 %collective-permute-start.31 = (bf16[4,256,256]{2,1,0:T(8,128)(2,1)}, bf16[4,256,256]{2,1,0:T(8,128)(2,1)S(1)}, u32[]{:S(2)}, u32[]{:S(2)}) collective-permute-start(bf16[4,256,256]{2,1,0:T(8,128)(2,1)} %bitcast_dynamic-update-slice_fusion.41), channel_id=1, source_target_pairs={{0,32},{8,40},{16,48},{24,56},{32,64},{40,72},{48,80},{56,88},{64,... | collective-permute-start | bytes 1572872 | tf_op jit(solution)/shard_map/ppermute | solution.py:57
  131.3 21.0 %collective-permute-start.32 = (bf16[4,256,256]{2,1,0:T(8,128)(2,1)}, bf16[4,256,256]{2,1,0:T(8,128)(2,1)}, u32[]{:S(2)}, u32[]{:S(2)}) collective-permute-start(bf16[4,256,256]{2,1,0:T(8,128)(2,1)} %bitcast_dynamic-update-slice_fusion.41), channel_id=1, source_target_pairs={{0,224},{8,232},{16,240},{24,248},{32,0},{40,8},{48,16},{56,24},{6... | collective-permute-start | bytes 1572872 | tf_op jit(solution)/shard_map/ppermute | solution.py:58
  146.8 24.9 %collective-permute-start.49 = (bf16[256,2048]{1,0:T(8,128)(2,1)}, bf16[256,2048]{1,0:T(8,128)(2,1)}, u32[]{:S(2)}, u32[]{:S(2)}) collective-permute-start(bf16[256,2048]{1,0:T(8,128)(2,1)} %param.22), channel_id=1, source_target_pairs={{0,4},{1,5},{2,6},{3,7},{4,0},{5,1},{6,2},{7,3},{8,12},{9,13},{10,... | collective-permute-start | bytes 3145736 | tf_op jit(solution)/shard_map/ppermute | solution.py:115
  152.3 42.0 %collective-permute-start.51 = (bf16[256,2048]{1,0:T(8,128)(2,1)}, bf16[256,2048]{1,0:T(8,128)(2,1)S(1)}, u32[]{:S(2)}, u32[]{:S(2)}) collective-permute-start(bf16[256,2048]{1,0:T(8,128)(2,1)} %param.22), channel_id=1, source_target_pairs={{0,6},{1,7},{2,0},{3,1},{4,2},{5,3},{6,4},{7,5},{8,14},{9,15},{10,... | collective-permute-start | bytes 3145736 | tf_op jit(solution)/shard_map/ppermute | solution.py:115
  155.0 40.7 %collective-permute-start.23 = (bf16[8,256,256]{2,1,0:T(8,128)(2,1)S(1)}, bf16[8,256,256]{2,1,0:T(8,128)(2,1)S(1)}, u32[]{:S(2)}, u32[]{:S(2)}) collective-permute-start(bf16[8,256,256]{2,1,0:T(8,128)(2,1)S(1)} %constant_dynamic-update-slice_fusion.16), channel_id=1, source_target_pairs={{0,8},{8,16},{16,24},{24,0},{32,40},{40,48},{48,56},{56,32},{64,72... | collective-permute-start | bytes 3145736 | tf_op jit(solution)/shard_map/ppermute | solution.py:57
  156.9 40.9 %collective-permute-start.24 = (bf16[8,256,256]{2,1,0:T(8,128)(2,1)S(1)}, bf16[8,256,256]{2,1,0:T(8,128)(2,1)S(1)}, u32[]{:S(2)}, u32[]{:S(2)}) collective-permute-start(bf16[8,256,256]{2,1,0:T(8,128)(2,1)S(1)} %constant_dynamic-update-slice_fusion.16), channel_id=1, source_target_pairs={{0,24},{8,0},{16,8},{24,16},{32,56},{40,32},{48,40},{56,48},{64,88... | collective-permute-start | bytes 3145736 | tf_op jit(solution)/shard_map/ppermute | solution.py:58
  161.5 32.8 %collective-permute-start.34 = (bf16[4,256,256]{2,1,0:T(8,128)(2,1)}, bf16[4,256,256]{2,1,0:T(8,128)(2,1)S(1)}, u32[]{:S(2)}, u32[]{:S(2)}) collective-permute-start(bf16[4,256,256]{2,1,0:T(8,128)(2,1)} %collective-permute-done.32), channel_id=1, source_target_pairs={{0,224},{8,232},{16,240},{24,248},{32,0},{40,8},{48,16},{56,24},{6... | collective-permute-start | bytes 1572872 | tf_op jit(solution)/shard_map/ppermute | solution.py:58
  171.7 42.9 %collective-permute-start.48 = (bf16[256,2048]{1,0:T(8,128)(2,1)}, bf16[256,2048]{1,0:T(8,128)(2,1)S(1)}, u32[]{:S(2)}, u32[]{:S(2)}) collective-permute-start(bf16[256,2048]{1,0:T(8,128)(2,1)} %collective-permute-done.47), channel_id=1, source_target_pairs={{0,1},{1,0},{2,3},{3,2},{4,5},{5,4},{6,7},{7,6},{8,9},{9,8},{10,11... | collective-permute-start | bytes 3145736 | tf_op jit(solution)/shard_map/ppermute | solution.py:116
  194.3 26.9 %collective-permute-start.50 = (bf16[256,2048]{1,0:T(8,128)(2,1)}, bf16[256,2048]{1,0:T(8,128)(2,1)S(1)}, u32[]{:S(2)}, u32[]{:S(2)}) collective-permute-start(bf16[256,2048]{1,0:T(8,128)(2,1)} %collective-permute-done.49), channel_id=1, source_target_pairs={{0,1},{1,0},{2,3},{3,2},{4,5},{5,4},{6,7},{7,6},{8,9},{9,8},{10,11... | collective-permute-start | bytes 3145736 | tf_op jit(solution)/shard_map/ppermute | solution.py:116
  194.3 29.4 %collective-permute-start.52 = (bf16[256,2048]{1,0:T(8,128)(2,1)S(1)}, bf16[256,2048]{1,0:T(8,128)(2,1)S(1)}, u32[]{:S(2)}, u32[]{:S(2)}) collective-permute-start(bf16[256,2048]{1,0:T(8,128)(2,1)S(1)} %collective-permute-done.51), channel_id=1, source_target_pairs={{0,1},{1,0},{2,3},{3,2},{4,5},{5,4},{6,7},{7,6},{8,9},{9,8},{10,11... | collective-permute-start | bytes 3145736 | tf_op jit(solution)/shard_map/ppermute | solution.py:116
  209.5 20.5 %collective-permute-start.25 = (bf16[4,256,256]{2,1,0:T(8,128)(2,1)S(1)}, bf16[4,256,256]{2,1,0:T(8,128)(2,1)S(1)}, u32[]{:S(2)}, u32[]{:S(2)}) collective-permute-start(bf16[4,256,256]{2,1,0:T(8,128)(2,1)S(1)} %slice.129), channel_id=1, source_target_pairs={{0,8},{8,16},{16,24},{24,0},{32,40},{40,48},{48,56},{56,32},{64,72... | collective-permute-start | bytes 1572872 | tf_op jit(solution)/shard_map/ppermute | solution.py:62
  212.6 17.4 %collective-permute-start.26 = (bf16[4,256,256]{2,1,0:T(8,128)(2,1)S(1)}, bf16[4,256,256]{2,1,0:T(8,128)(2,1)S(1)}, u32[]{:S(2)}, u32[]{:S(2)}) collective-permute-start(bf16[4,256,256]{2,1,0:T(8,128)(2,1)S(1)} %slice.130), channel_id=1, source_target_pairs={{0,24},{8,0},{16,8},{24,16},{32,56},{40,32},{48,40},{56,48},{64,88... | collective-permute-start | bytes 1572872 | tf_op jit(solution)/shard_map/ppermute | solution.py:63
  230.2 23.5 %collective-permute-start.53 = (bf16[64,512]{1,0:T(8,128)(2,1)S(1)}, bf16[64,512]{1,0:T(8,128)(2,1)S(1)}, u32[]{:S(2)}, u32[]{:S(2)}) collective-permute-start(bf16[64,512]{1,0:T(8,128)(2,1)S(1)} %get-tuple-element.157), channel_id=1, source_target_pairs={{0,32},{8,40},{16,48},{24,56},{32,64},{40,72},{48,80},{56,88},{64,... | collective-permute-start | bytes 196616 | tf_op jit(solution)/shard_map/ppermute | solution.py:57
  230.2 24.4 %collective-permute-start.54 = (bf16[64,512]{1,0:T(8,128)(2,1)S(1)}, bf16[64,512]{1,0:T(8,128)(2,1)S(1)}, u32[]{:S(2)}, u32[]{:S(2)}) collective-permute-start(bf16[64,512]{1,0:T(8,128)(2,1)S(1)} %get-tuple-element.157), channel_id=1, source_target_pairs={{0,224},{8,232},{16,240},{24,248},{32,0},{40,8},{48,16},{56,24},{6... | collective-permute-start | bytes 196616 | tf_op jit(solution)/shard_map/ppermute | solution.py:58
  249.1 44.9 %collective-permute-start.39 = (bf16[256,256]{1,0:T(8,128)(2,1)S(1)}, bf16[256,256]{1,0:T(8,128)(2,1)S(1)}, u32[]{:S(2)}, u32[]{:S(2)}) collective-permute-start(bf16[256,256]{1,0:T(8,128)(2,1)S(1)} %copy.76), channel_id=1, source_target_pairs={{0,1},{1,0},{2,3},{3,2},{4,5},{5,4},{6,7},{7,6},{8,9},{9,8},{10,11... | collective-permute-start | bytes 393224 | tf_op jit(solution)/shard_map/ppermute | solution.py:116
  249.2 45.1 %collective-permute-start.40 = (bf16[256,256]{1,0:T(8,128)(2,1)S(1)}, bf16[256,256]{1,0:T(8,128)(2,1)S(1)}, u32[]{:S(2)}, u32[]{:S(2)}) collective-permute-start(bf16[256,256]{1,0:T(8,128)(2,1)S(1)} %copy.76), channel_id=1, source_target_pairs={{0,2},{1,3},{2,4},{3,5},{4,6},{5,7},{6,0},{7,1},{8,10},{9,11},{10,... | collective-permute-start | bytes 393224 | tf_op jit(solution)/shard_map/ppermute | solution.py:115
  251.1 58.1 %collective-permute-start.42 = (bf16[256,256]{1,0:T(8,128)(2,1)S(1)}, bf16[256,256]{1,0:T(8,128)(2,1)S(1)}, u32[]{:S(2)}, u32[]{:S(2)}) collective-permute-start(bf16[256,256]{1,0:T(8,128)(2,1)S(1)} %copy.76), channel_id=1, source_target_pairs={{0,4},{1,5},{2,6},{3,7},{4,0},{5,1},{6,2},{7,3},{8,12},{9,13},{10,... | collective-permute-start | bytes 393224 | tf_op jit(solution)/shard_map/ppermute | solution.py:115
  253.6 55.6 %collective-permute-start.44 = (bf16[256,256]{1,0:T(8,128)(2,1)S(1)}, bf16[256,256]{1,0:T(8,128)(2,1)S(1)}, u32[]{:S(2)}, u32[]{:S(2)}) collective-permute-start(bf16[256,256]{1,0:T(8,128)(2,1)S(1)} %copy.76), channel_id=1, source_target_pairs={{0,6},{1,7},{2,0},{3,1},{4,2},{5,3},{6,4},{7,5},{8,14},{9,15},{10,... | collective-permute-start | bytes 393224 | tf_op jit(solution)/shard_map/ppermute | solution.py:115
  291.0 35.5 %collective-permute-start.69 = (bf16[4,64,512]{2,1,0:T(8,128)(2,1)S(1)}, bf16[4,64,512]{2,1,0:T(8,128)(2,1)S(1)}, u32[]{:S(2)}, u32[]{:S(2)}) collective-permute-start(bf16[4,64,512]{2,1,0:T(8,128)(2,1)S(1)} %bitcast_dynamic-update-slice_fusion.43), channel_id=1, source_target_pairs={{0,32},{8,40},{16,48},{24,56},{32,64},{40,72},{48,80},{56,88},{64,... | collective-permute-start | bytes 786440 | tf_op jit(solution)/shard_map/ppermute | solution.py:57
  293.9 34.7 %collective-permute-start.70 = (bf16[4,64,512]{2,1,0:T(8,128)(2,1)S(1)}, bf16[4,64,512]{2,1,0:T(8,128)(2,1)S(1)}, u32[]{:S(2)}, u32[]{:S(2)}) collective-permute-start(bf16[4,64,512]{2,1,0:T(8,128)(2,1)S(1)} %bitcast_dynamic-update-slice_fusion.43), channel_id=1, source_target_pairs={{0,224},{8,232},{16,240},{24,248},{32,0},{40,8},{48,16},{56,24},{6... | collective-permute-start | bytes 786440 | tf_op jit(solution)/shard_map/ppermute | solution.py:58
  316.8 22.9 %collective-permute-start.61 = (bf16[8,64,512]{2,1,0:T(8,128)(2,1)S(1)}, bf16[8,64,512]{2,1,0:T(8,128)(2,1)S(1)}, u32[]{:S(2)}, u32[]{:S(2)}) collective-permute-start(bf16[8,64,512]{2,1,0:T(8,128)(2,1)S(1)} %bitcast_dynamic-update-slice_fusion.45), channel_id=1, source_target_pairs={{0,8},{8,16},{16,24},{24,0},{32,40},{40,48},{48,56},{56,32},{64,72... | collective-permute-start | bytes 1572872 | tf_op jit(solution)/shard_map/ppermute | solution.py:57
  316.9 22.9 %collective-permute-start.62 = (bf16[8,64,512]{2,1,0:T(8,128)(2,1)S(1)}, bf16[8,64,512]{2,1,0:T(8,128)(2,1)S(1)}, u32[]{:S(2)}, u32[]{:S(2)}) collective-permute-start(bf16[8,64,512]{2,1,0:T(8,128)(2,1)S(1)} %bitcast_dynamic-update-slice_fusion.45), channel_id=1, source_target_pairs={{0,24},{8,0},{16,8},{24,16},{32,56},{40,32},{48,40},{56,48},{64,88... | collective-permute-start | bytes 1572872 | tf_op jit(solution)/shard_map/ppermute | solution.py:58
  339.7 15.3 %collective-permute-start.63 = (bf16[4,64,512]{2,1,0:T(8,128)(2,1)S(1)}, bf16[4,64,512]{2,1,0:T(8,128)(2,1)S(1)}, u32[]{:S(2)}, u32[]{:S(2)}) collective-permute-start(bf16[4,64,512]{2,1,0:T(8,128)(2,1)S(1)} %slice.144), channel_id=1, source_target_pairs={{0,8},{8,16},{16,24},{24,0},{32,40},{40,48},{48,56},{56,32},{64,72... | collective-permute-start | bytes 786440 | tf_op jit(solution)/shard_map/ppermute | solution.py:62
  339.8 15.9 %collective-permute-start.64 = (bf16[4,64,512]{2,1,0:T(8,128)(2,1)S(1)}, bf16[4,64,512]{2,1,0:T(8,128)(2,1)S(1)}, u32[]{:S(2)}, u32[]{:S(2)}) collective-permute-start(bf16[4,64,512]{2,1,0:T(8,128)(2,1)S(1)} %slice.145), channel_id=1, source_target_pairs={{0,24},{8,0},{16,8},{24,16},{32,56},{40,32},{48,40},{56,48},{64,88... | collective-permute-start | bytes 786440 | tf_op jit(solution)/shard_map/ppermute | solution.py:63
  (70 other events, 719.4 us)
Sparse Core Ops, SparseCore 0:
  17.9 106.4 all-gather.1
